TPU v7x, 256 devices: a whole 4x4x8 slice. The times are simulated.
256 devices in a mesh: dp: 8 (over x, core), seq: 32 (over z, y).
Axes of the slice: x: 4, y: 4, z: 8, core: 2. Of those that a mesh axis runs over, the one named last changes fastest.
Arguments:
- features: bfloat16 [8, 4096, 2048], P('dp', 'seq'), may hold values from -6 to 6
- queries: bfloat16 [8, 4096, 2048], P('dp', 'seq'), may hold values from -4.5 to 4.5
- key_rows: bfloat16 [8, 4096, 2048], P('dp', 'seq'), may hold values from -4.5 to 4.5
- value_rows: bfloat16 [8, 4096, 2048], P('dp', 'seq'), may hold values from -6 to 6
- cotangent: bfloat16 [8, 4096, 2048], P('dp', 'seq'), may hold values from -6 to 6
- global_queries: bfloat16 [8, 64, 2048], P('dp'), may hold values from -4.5 to 4.5
- global_keys: bfloat16 [8, 64, 2048], P('dp'), may hold values from -4.5 to 4.5
- global_values: bfloat16 [8, 64, 2048], P('dp'), may hold values from -6 to 6
- random_blocks: int32 [8, 64, 3], P('dp'), may hold values from 0 to 63, as said below
Outputs:
- attended: bfloat16 [8, 4096, 2048], P('dp', 'seq')
- global_attended: bfloat16 [8, 64, 2048], P('dp')
- weight_grad: float32 [2048, 2048], P(('dp', 'seq'))
Inputs may be any that keep to these rules, and one draw needn't show every extreme that they name: `random_blocks`: block b of a document lies on seq device b // 2. The 6 random blocks named by the 2 query blocks of one device lie on 6 different devices.
All inputs are finite; a program needn't handle non-finite values.
Results may differ from a plain program's by a relative error of at most 0.025.
Values may be sent and summed in bfloat16 or wider, within the bound.
A program may use at most 192 MiB of HBM per device.

v0:
```python
import math

import jax
import jax.numpy as jnp
from jax import lax
from jax.sharding import PartitionSpec as P

HEADS = 16
HEAD_DIM = 128
G = 64
BLOCK = 64
R = 3


NEGATIVE = -1e30


def padded_2(array, sides, width):
    for axis, dim in sides:
        count, length = (lax.axis_size(axis), array.shape[dim])
        up = [(i, (i + 1) % count) for i in range(count - 1)]
        down = [(j, i) for i, j in up]
        last = lax.slice_in_dim(array, length - width, length, axis=dim)
        leading = lax.slice_in_dim(array, 0, width, axis=dim)
        before = lax.ppermute(last, axis, up)
        after = lax.ppermute(leading, axis, down)
        array = jnp.concatenate([before, array, after], axis=dim)
    return array


def merged_2(part, axis, combine):
    gathered = jax.tree.map(lambda a: lax.all_gather(a, axis), part)

    def take(source):
        return jax.tree.map(lambda a: lax.dynamic_index_in_dim(a, source, 0, False), gathered)

    return lax.fori_loop(
        1, lax.axis_size(axis), lambda source, state: combine(state, take(source)), take(0)
    )


def combine(earlier_part, later_part):
    earlier_peak, earlier_mass, earlier_values = earlier_part
    later_peak, later_mass, later_values = later_part
    top_score = jnp.maximum(earlier_peak, later_peak)
    earlier_weight = jnp.exp(earlier_peak - top_score)
    later_weight = jnp.exp(later_peak - top_score)
    total_mass = earlier_mass * earlier_weight + later_mass * later_weight
    value_sum = (
        earlier_values * earlier_weight.T[:, :, None] + later_values * later_weight.T[:, :, None]
    )
    return (top_score, total_mass, value_sum)


def span_partial(global_heads, span_keys, span_values, scaling):
    scores = (
        jnp.einsum("ghe,the->hgt", global_heads, span_keys, preferred_element_type=jnp.float32)
        * scaling
    )
    peak_score = jnp.max(scores, axis=-1)
    exp_weights = jnp.exp(scores - peak_score[..., None])
    total_mass = jnp.sum(exp_weights, axis=-1)
    value_part = jnp.einsum(
        "hgt,the->ghe",
        exp_weights.astype(jnp.bfloat16),
        span_values,
        preferred_element_type=jnp.float32,
    )
    return (peak_score, total_mass, value_part)


def per_device(
    features,
    queries,
    key_rows,
    value_rows,
    cotangent,
    global_queries,
    global_keys,
    global_values,
    random_blocks,
):
    scaling = 1.0 / math.sqrt(HEAD_DIM)
    length_dev = queries.shape[1]
    width = queries.shape[2]
    blocks_dev = length_dev // BLOCK
    devices = lax.axis_size("seq")
    position = lax.axis_index("seq")
    request_count = blocks_dev * R
    capacity = (request_count + devices - 1) // devices
    total_blocks = devices * blocks_dev
    stacked = jnp.stack([key_rows[0], value_rows[0]], axis=1)
    padded = padded_2(stacked, (("seq", 0),), BLOCK)
    padded_blocks = padded.reshape(blocks_dev + 2, BLOCK, 2, HEADS, HEAD_DIM)
    window = jnp.concatenate([padded_blocks[:-2], padded_blocks[1:-1], padded_blocks[2:]], axis=1)
    all_requests = random_blocks[0].reshape(devices, request_count)
    owners = all_requests // blocks_dev
    within = all_requests % blocks_dev
    request_order = jnp.arange(request_count)
    earlier_mask = request_order[None, :] < request_order[:, None]
    same_owner = owners[:, :, None] == owners[:, None, :]
    slot_ranks = jnp.sum(same_owner & earlier_mask[None], axis=-1)
    slot_numbers = jnp.arange(capacity)
    wanted = (owners == position)[:, None, :] & (
        slot_ranks[:, None, :] == slot_numbers[None, :, None]
    )
    local_index = jnp.sum(jnp.where(wanted, within[:, None, :], 0), axis=-1)
    own_blocks = stacked.reshape(blocks_dev, BLOCK, 2, width)
    outgoing = own_blocks[local_index]
    incoming = lax.all_to_all(outgoing, "seq", split_axis=0, concat_axis=0, tiled=True)
    my_owners = lax.dynamic_index_in_dim(owners, position, 0, keepdims=False)
    my_ranks = lax.dynamic_index_in_dim(slot_ranks, position, 0, keepdims=False)
    flat_index = my_owners * capacity + my_ranks
    fetched = incoming.reshape(devices * capacity, BLOCK, 2, width)[flat_index]
    random_side = fetched.reshape(blocks_dev, R * BLOCK, 2, HEADS, HEAD_DIM)
    window_keys = window[:, :, 0]
    window_values = window[:, :, 1]
    random_keys = random_side[:, :, 0]
    random_values = random_side[:, :, 1]
    glob_keys = global_keys[0].reshape(G, HEADS, HEAD_DIM)
    glob_values = global_values[0].reshape(G, HEADS, HEAD_DIM)
    query_blocks = queries[0].reshape(blocks_dev, BLOCK, HEADS, HEAD_DIM)
    block_number = position * blocks_dev + jnp.arange(blocks_dev)[:, None]
    column = jnp.arange(3 * BLOCK)[None, :]
    valid_keys = ((column >= BLOCK) | (block_number > 0)) & (
        (column < 2 * BLOCK) | (block_number < total_blocks - 1)
    )
    window_scores = (
        jnp.einsum("jqhe,jkhe->jhqk", query_blocks, window_keys, preferred_element_type=jnp.float32)
        * scaling
    )
    window_scores = jnp.where(valid_keys[:, None, None, :], window_scores, NEGATIVE)
    random_scores = (
        jnp.einsum("jqhe,jkhe->jhqk", query_blocks, random_keys, preferred_element_type=jnp.float32)
        * scaling
    )
    global_scores = (
        jnp.einsum("jqhe,khe->jhqk", query_blocks, glob_keys, preferred_element_type=jnp.float32)
        * scaling
    )
    scores = jnp.concatenate([window_scores, random_scores, global_scores], axis=-1)
    peak_score = jnp.max(scores, axis=-1, keepdims=True)
    exp_weights = jnp.exp(scores - peak_score)
    soft_weights = exp_weights / jnp.sum(exp_weights, axis=-1, keepdims=True)
    low_weights = soft_weights.astype(jnp.bfloat16)
    split_one = 3 * BLOCK
    split_two = 3 * BLOCK + R * BLOCK
    combined = jnp.einsum(
        "jhqk,jkhe->jqhe",
        low_weights[..., :split_one],
        window_values,
        preferred_element_type=jnp.float32,
    )
    combined = combined + jnp.einsum(
        "jhqk,jkhe->jqhe",
        low_weights[..., split_one:split_two],
        random_values,
        preferred_element_type=jnp.float32,
    )
    combined = combined + jnp.einsum(
        "jhqk,khe->jqhe",
        low_weights[..., split_two:],
        glob_values,
        preferred_element_type=jnp.float32,
    )
    attended = combined.reshape(length_dev, width).astype(jnp.bfloat16)
    global_heads = global_queries[0].reshape(G, HEADS, HEAD_DIM)
    local_peak, local_mass, local_values = span_partial(
        global_heads,
        key_rows[0].reshape(length_dev, HEADS, HEAD_DIM),
        value_rows[0].reshape(length_dev, HEADS, HEAD_DIM),
        scaling,
    )
    merged = merged_2((local_peak, local_mass, local_values), "seq", combine)
    own_part = span_partial(global_heads, glob_keys, glob_values, scaling)
    final_peak, final_mass, final_values = combine(merged, own_part)
    global_attended = (
        (final_values / final_mass.T[:, :, None]).reshape(G, width).astype(jnp.bfloat16)
    )
    grad_rows = cotangent[0]
    grad_blocks = grad_rows.reshape(blocks_dev, BLOCK, HEADS, HEAD_DIM)
    delta_rows = jnp.sum(
        (grad_rows.astype(jnp.float32) * attended.astype(jnp.float32)).reshape(
            blocks_dev, BLOCK, HEADS, HEAD_DIM
        ),
        axis=-1,
    )
    grad_weights = jnp.concatenate(
        [
            jnp.einsum(
                "jqhe,jkhe->jhqk", grad_blocks, window_values, preferred_element_type=jnp.float32
            ),
            jnp.einsum(
                "jqhe,jkhe->jhqk", grad_blocks, random_values, preferred_element_type=jnp.float32
            ),
            jnp.einsum(
                "jqhe,khe->jhqk", grad_blocks, glob_values, preferred_element_type=jnp.float32
            ),
        ],
        axis=-1,
    )
    grad_scores = (
        soft_weights * (grad_weights - jnp.transpose(delta_rows, (0, 2, 1))[..., None])
    ).astype(jnp.bfloat16)
    grad_query = jnp.einsum(
        "jhqk,jkhe->jqhe",
        grad_scores[..., :split_one],
        window_keys,
        preferred_element_type=jnp.float32,
    )
    grad_query = grad_query + jnp.einsum(
        "jhqk,jkhe->jqhe",
        grad_scores[..., split_one:split_two],
        random_keys,
        preferred_element_type=jnp.float32,
    )
    grad_query = grad_query + jnp.einsum(
        "jhqk,khe->jqhe",
        grad_scores[..., split_two:],
        glob_keys,
        preferred_element_type=jnp.float32,
    )
    query_grad = (grad_query * scaling).reshape(length_dev, width).astype(jnp.bfloat16)
    feature_rows = features[0]
    width_in = feature_rows.shape[1]
    data_devices = lax.axis_size("dp")
    slice_rows = width_in // (data_devices * devices)
    permuted = feature_rows.reshape(length_dev, data_devices, devices, slice_rows)
    permuted = permuted.transpose(0, 2, 1, 3).reshape(length_dev, width_in)
    summed_rows = lax.psum_scatter(
        lax.dot_general(
            permuted, query_grad, (((0,), (0,)), ((), ())), preferred_element_type=jnp.float32
        ),
        "seq",
        scatter_dimension=0,
        tiled=True,
    )
    weight_grad = lax.psum_scatter(summed_rows, "dp", scatter_dimension=0, tiled=True)
    return (attended[None], global_attended[None], weight_grad)


def solution(mesh):
    placed = (
        P("dp", "seq", None),
        P("dp", "seq", None),
        P("dp", "seq", None),
        P("dp", "seq", None),
        P("dp", "seq", None),
        P("dp", None, None),
        P("dp", None, None),
        P("dp", None, None),
        P("dp", None, None),
    )
    return jax.shard_map(
        per_device,
        mesh=mesh,
        in_specs=placed,
        out_specs=(P("dp", "seq", None), P("dp", None, None), P(("dp", "seq"), None)),
        check_vma=False,
    )
```

profile of v0, /device:TPU:1, one launch (start us, length us, event | category | flops | bytes accessed | tf_op | source)
XLA Modules:
  0.0 882.1 jit_solution(10121550841686970311)
XLA Ops:
  8.4 1.3 pad_maximum_fusion.5
  9.7 7.1 gather_fusion
  16.8 12.2 %all-to-all-start = ((bf16[32,1,64,2,2048]{4,2,3,1,0:T(8,128)(2,1)}), bf16[32,1,64,2,2048]{4,2,3,1,0:T(8,128)(2,1)}, u32[]{:S(2)}, u32[]{:S(2)}) async-start(bf16[32,1,64,2,2048]{4,2,3,1,0:T(8,128)(2,1)} %bitcast.218), calls=%async_computation | async-start | bytes 33554432 | tf_op jit(solution)/shard_map/all_to_all | solution.py:110
  31.5 1.2 convolution_bitcast_fusion.7
  33.8 3.9 collective-permute-start
  37.7 1.3 collective-permute-start.1
  41.2 1.7 copy.269
  43.1 1.3 fusion.62
  44.9 1.3 convolution_bitcast_fusion.4
  48.0 1.3 copy.251
  51.4 43.6 %collective-permute-done = bf16[64,2,2048]{2,0,1:T(8,128)(2,1)} collective-permute-done((bf16[64,2,2048]{2,0,1:T(8,128)(2,1)}, bf16[64,2,2048]{2,0,1:T(8,128)(2,1)}, u32[]{:S(2)}, u32[]{:S(2)}) %collective-permute-start) | collective-permute-done | bytes 524320 | tf_op jit(solution)/shard_map/ppermute | solution.py:25
  95.0 20.4 %collective-permute-done.1 = bf16[64,2,2048]{2,0,1:T(8,128)(2,1)} collective-permute-done((bf16[64,2,2048]{2,0,1:T(8,128)(2,1)}, bf16[64,2,2048]{2,0,1:T(8,128)(2,1)}, u32[]{:S(2)}, u32[]{:S(2)}) %collective-permute-start.1) | collective-permute-done | bytes 524320 | tf_op jit(solution)/shard_map/ppermute | solution.py:26
  115.5 1.3 pad_maximum_fusion.3
  119.6 2.4 convolution_bitcast_fusion.2
  122.0 2.5 fusion.81
  124.6 370.2 %all-to-all-done = bf16[32,1,64,2,2048]{4,2,3,1,0:T(8,128)(2,1)} async-done(((bf16[32,1,64,2,2048]{4,2,3,1,0:T(8,128)(2,1)}), bf16[32,1,64,2,2048]{4,2,3,1,0:T(8,128)(2,1)}, u32[]{:S(2)}, u32[]{:S(2)}) %all-to-all-start) | async-done | bytes 16777248 | tf_op jit(solution)/shard_map/all_to_all | solution.py:110
  494.7 8.2 gather_fusion.1
  503.0 2.3 copy.224
  507.3 1.2 fusion.82
  509.2 2.1 fusion.9
  511.3 2.3 fusion.79
  515.5 1.2 multiply_reduce_fusion
  516.6 1.1 convolution_bitcast_fusion.1
  518.5 3.7 fusion.8
  524.7 8.1 convolution_bitcast_fusion
  532.8 17.6 %copy.255 = f32[2048,2048]{1,0:T(8,128)} copy(f32[2048,2048]{0,1:T(8,128)} %convolution_bitcast_fusion) | data formatting | bytes 33554432
  550.4 61.7 %all-gather = f32[512,64]{1,0:T(8,128)S(1)} all-gather(f32[16,64]{1,0:T(8,128)S(1)} %get-tuple-element.275), channel_id=2, replica_groups=mesh['dp'=8,'seq'=32] {'seq'}, dimensions={0}, use_global_device_ids=true | all-gather | bytes 135168 | tf_op jit(solution)/shard_map/all_gather | solution.py:32
  612.5 38.8 %all-gather.1 = f32[512,64]{1,0:T(8,128)S(1)} all-gather(f32[16,64]{1,0:T(8,128)S(1)} %fusion.40), channel_id=3, replica_groups=mesh['dp'=8,'seq'=32] {'seq'}, dimensions={0}, use_global_device_ids=true | all-gather | bytes 135168 | tf_op jit(solution)/shard_map/all_gather | solution.py:32
  653.1 160.0 %reduce-scatter.7.cloned.1.call-done = f32[64,2048]{1,0:T(8,128)} async-done(((f32[2048,2048]{1,0:T(8,128)}), f32[64,2048]{1,0:T(8,128)}) %reduce-scatter.7.cloned.1.call-update) | async-done | bytes 524304
  813.1 59.4 %while.19 = (s32[]{:T(128)}, f32[16,64]{1,0:T(8,128)S(1)}, f32[16,64]{1,0:T(8,128)S(1)}, f32[64,16,128]{2,1,0:T(8,128)S(1)}, f32[32,16,64]{2,1,0:T(8,128)S(1)}, ...) while((s32[]{:T(128)}, f32[16,64]{1,0:T(8,128)S(1)}, ...), condition=%wide.region_9.10_spmd, body=%wide.region_8.9_spmd.sunk | while | flops 400389 | bytes 2699419 | solution.py:37
  813.2 1.1 constant_dynamic-slice_fusion.2
  815.2 1.1 constant_dynamic-slice_fusion.2
  817.1 1.1 constant_dynamic-slice_fusion.2
  819.0 1.1 constant_dynamic-slice_fusion.2
  828.6 1.1 constant_dynamic-slice_fusion.2
  830.5 1.1 constant_dynamic-slice_fusion.2
  832.4 1.1 constant_dynamic-slice_fusion.2
  834.3 1.1 constant_dynamic-slice_fusion.2
  836.2 1.1 constant_dynamic-slice_fusion.2
  838.2 1.1 constant_dynamic-slice_fusion.2
  842.0 1.1 constant_dynamic-slice_fusion.2
  843.9 1.1 constant_dynamic-slice_fusion.2
  847.7 1.1 constant_dynamic-slice_fusion.2
  849.7 1.1 constant_dynamic-slice_fusion.2
  857.3 1.1 constant_dynamic-slice_fusion.2
  859.2 1.1 constant_dynamic-slice_fusion.2
  861.2 1.1 constant_dynamic-slice_fusion.2
  870.7 1.1 constant_dynamic-slice_fusion.2
  (321 shorter events, 65.3 us)
Async XLA Ops:
  16.8 12.3 %copy-start.6 = (bf16[1,128,2048]{2,1,0:T(8,128)(2,1)S(1)}, bf16[1,128,2048]{2,1,0:T(8,128)(2,1)}, u32[]{:S(2)}) copy-start(bf16[1,128,2048]{2,1,0:T(8,128)(2,1)} %param.14) | copy-start | bytes 1572868
  16.8 12.4 %copy-start.7 = (bf16[1,128,2048]{2,1,0:T(8,128)(2,1)S(1)}, bf16[1,128,2048]{2,1,0:T(8,128)(2,1)}, u32[]{:S(2)}) copy-start(bf16[1,128,2048]{2,1,0:T(8,128)(2,1)} %param.13) | copy-start | bytes 1572868
  16.8 478.0 %all-to-all-start = ((bf16[32,1,64,2,2048]{4,2,3,1,0:T(8,128)(2,1)}), bf16[32,1,64,2,2048]{4,2,3,1,0:T(8,128)(2,1)}, u32[]{:S(2)}, u32[]{:S(2)}) async-start(bf16[32,1,64,2,2048]{4,2,3,1,0:T(8,128)(2,1)} %bitcast.218), calls=%async_computation | async-start | bytes 33554432 | tf_op jit(solution)/shard_map/all_to_all | solution.py:110
  29.0 1.0 copy-start.27
  29.0 622.7 %all-gather.5.cloned.1.call-start = ((), (), s32[]{:S(2)}) async-start(), calls=%async_computation.3 | async-start | bytes 17301504 | tf_op jit(solution)/shard_map/all_gather | solution.py:32
  29.3 0.8 copy-start.10
  30.0 0.7 copy-start.16
  30.7 0.8 copy-start.8
  31.5 7.5 copy-start.25
  32.7 6.4 copy-start.26
  32.7 780.4 %reduce-scatter.7.cloned.1.call-start = ((), (), s32[]{:S(2)}) async-start(), calls=%async_computation.4 | async-start | bytes 17301504
  33.8 61.2 %collective-permute-start = (bf16[64,2,2048]{2,0,1:T(8,128)(2,1)}, bf16[64,2,2048]{2,0,1:T(8,128)(2,1)}, u32[]{:S(2)}, u32[]{:S(2)}) collective-permute-start(bf16[64,2,2048]{2,0,1:T(8,128)(2,1)} %get-tuple-element.266), channel_id=1, source_target_pairs={{0,1},{1,2},{2,3},{3,4},{4,5},{5,6},{6,7},{7,8},{8,9},{9,10},{10,1... | collective-permute-start | bytes 1572872 | tf_op jit(solution)/shard_map/ppermute | solution.py:25
  37.7 77.8 %collective-permute-start.1 = (bf16[64,2,2048]{2,0,1:T(8,128)(2,1)}, bf16[64,2,2048]{2,0,1:T(8,128)(2,1)}, u32[]{:S(2)}, u32[]{:S(2)}) collective-permute-start(bf16[64,2,2048]{2,0,1:T(8,128)(2,1)} %get-tuple-element.267), channel_id=1, source_target_pairs={{1,0},{2,1},{3,2},{4,3},{5,4},{6,5},{7,6},{8,7},{9,8},{10,9},{11,1... | collective-permute-start | bytes 1572872 | tf_op jit(solution)/shard_map/ppermute | solution.py:26
  39.1 5.7 copy-start.2
  39.2 3.9 copy-start.12
  42.9 1.9 copy-start.18
  44.5 2.6 copy-start.11
  117.3 1.0 copy-start.22
  117.3 1.2 copy-start.23
  118.5 1.0 copy-start.3
  119.6 2.5 copy-start.13
  506.3 1.0 copy-start.14
  507.3 1.6 copy-start
  507.3 1.9 copy-start.1
  514.3 1.0 copy-start.4
  514.4 1.1 copy-start.19
  516.6 1.6 copy-start.5
  516.6 1.9 copy-start.15
  523.7 1.0 copy-start.21
  550.4 61.7 %copy-start.9 = (f32[16,64,128]{2,1,0:T(8,128)S(1)}, f32[16,64,128]{2,1,0:T(8,128)}, u32[]{:S(2)}) copy-start(f32[16,64,128]{2,1,0:T(8,128)} %copy-done.8) | copy-start | bytes 1572868
  550.4 100.9 %copy-start.17 = (bf16[8,8,16,128]{3,2,1,0:T(8,128)(2,1)S(1)}, bf16[8,8,16,128]{3,2,1,0:T(8,128)(2,1)}, u32[]{:S(2)}) copy-start(bf16[8,8,16,128]{3,2,1,0:T(8,128)(2,1)} %copy-done.16) | copy-start | bytes 786436
  550.4 325.2 %reduce-scatter.9.cloned.1.call-start = ((), (), s32[]{:S(2)}) async-start(), calls=%async_computation.5 | async-start | bytes 589824
  813.1 59.5 %copy-start.24 = (bf16[2,64,16,128]{3,1,2,0:T(8,128)(2,1)S(1)}, bf16[2,64,16,128]{3,1,2,0:T(8,128)(2,1)}, u32[]{:S(2)}) copy-start(bf16[2,64,16,128]{3,1,2,0:T(8,128)(2,1)} %get-tuple-element.280) | copy-start | bytes 1572868
  872.6 1.4 copy-start.20
Sparse Core Ops, SparseCore 0:
  32.8 420.5 all-gather.4
  550.5 262.5 reduce-scatter.6
  816.2 33.8 reduce-scatter.8
where the time goes:
time: 888 us; the launch traced here: 882 us
  waiting for transfers between devices  594 us (67%)
  blocking collectives  100 us (11%)
  local copies, waits for them, and re-layouts  95.9 us (11%)
  other arithmetic  33.2 us (4%)
  matrix products  25 us (3%)
  starting transfers between devices  17.5 us (2%)
  between operations  14.3 us (2%)
    all_to_all x1, waiting for transfers between devices, per_device(): lax.all_to_all(outgoing, 'seq', split_axis=0, concat_axis=0, tiled=True)  370 us
    unnamed x5, waiting for transfers between devices  160 us
    all_gather x2, blocking collectives, merged_2(): gathered = jax.tree.map(lambda a: lax.all_gather(a, axis), part)  100 us
    ppermute x1, waiting for transfers between devices, padded_2(): before = lax.ppermute(last, axis, up)  43.6 us
    dynamic_slice x34, local copies, waits for them, and re-layouts, take(): lax.dynamic_index_in_dim(a, source, 0, False)  34.9 us
    unnamed x69, local copies, waits for them, and re-layouts  30 us
    ppermute x1, waiting for transfers between devices, padded_2(): after = lax.ppermute(leading, axis, down)  20.4 us
    add x31, other arithmetic, combine(): earlier_values * earlier_weight.T[:, :, None]  17.8 us
  transfers between devices with their start and end apart: 6, of which 4 were waited for; matrix products, arithmetic and copies ran while one was open for 16% of the time, Pallas kernels for 0%

commit v1 on v0

v1 whole, which is shorter than its diff:
```python
import functools
import math

import jax
import jax.numpy as jnp
from jax import lax
from jax.experimental import pallas as pl
from jax.experimental.pallas import tpu as pltpu
from jax.sharding import PartitionSpec as P

E = 128
BLOCK = 64
R = 3
NY = 4
NC = 2
NEGATIVE = -1e30
MESH = pl.DeviceIdType.MESH
ANY = pl.BlockSpec(memory_space=pl.ANY)


def place(seqs):
    d, s = lax.axis_index("dp"), lax.axis_index("seq")
    return d, s, d // NC, d % NC, s // NY, s % NY


def head_columns(h):
    return pl.ds(pl.multiple_of(h * E, E), E)


def remote(src, dst, send, recv, d, s):
    return pltpu.make_async_remote_copy(
        src_ref=src, dst_ref=dst, send_sem=send, recv_sem=recv, device_id=(d, s), device_id_type=MESH
    )


def signal(sem, d, s):
    pl.semaphore_signal(sem, inc=1, device_id=(d, s), device_id_type=MESH)


def shuffle_kernel(seqs, xs, *refs):
    q, k, v, g, f, gq, gk, gv, rb = refs[:9]
    qo, ko, vo, go, fo, gqo, gko, gvo, rbo = refs[9:18]
    a_send, a_recv, b_send, b_recv, f_send, f_recv, c_send, c_recv = refs[18:]
    d, s, x, c, z, y = place(seqs)
    half = seqs // 2
    heads = half
    tokens = s // half
    slot = s % half
    sibling = x * NC + (1 - c)
    owner = z % NC
    mine = jnp.logical_and(owner == c, tokens == c)

    barrier = pltpu.get_barrier_semaphore()

    def greet(i, carry):
        source = c * half + i

        @pl.when(jnp.logical_not(jnp.logical_and(owner == c, source == s)))
        def _():
            signal(barrier, x * NC + owner, source)

        return carry

    lax.fori_loop(0, half, greet, 0)
    signal(barrier, sibling, s)

    def greet_f(i, carry):
        to_x, to_y = (x + i // NY) % xs, (y + i) % NY
        signal(barrier, to_x * NC + c, z * NY + to_y)
        return carry

    lax.fori_loop(1, xs * NY, greet_f, 0)

    @pl.when(mine)
    def _():
        pl.semaphore_wait(barrier, half + xs * NY - 1)

    @pl.when(jnp.logical_not(mine))
    def _():
        pl.semaphore_wait(barrier, half + xs * NY)

    def target(i):
        h = (i + s) % heads
        return h, ((h // NY) * NC + c) * NY + h % NY

    def pieces(h):
        columns = head_columns(h)
        return (
            (k.at[0, :, columns], ko.at[s]),
            (v.at[0, :, columns], vo.at[s]),
            (q.at[0, :, columns], qo.at[slot]),
            (g.at[0, :, columns], go.at[slot]),
        )

    def send(n):
        def body(i, carry):
            h, to = target(i)
            src, dst = pieces(h)[n]
            here = jnp.logical_and(mine, to == s)

            @pl.when(here)
            def _():
                pltpu.make_async_copy(src, dst, a_recv.at[n]).start()

            @pl.when(jnp.logical_not(here))
            def _():
                remote(src, dst, a_send.at[n], a_recv.at[n], x * NC + tokens, to).start()

            return carry

        lax.fori_loop(0, heads, body, 0)

    send(0)
    send(1)

    my_head = (z // NC) * NY + y
    columns = head_columns(my_head)
    rows = gqo.shape[0]
    shared = (
        (gq.at[0, pl.ds(pl.multiple_of(c * rows, rows), rows), columns],
         gq.at[0, pl.ds(pl.multiple_of((1 - c) * rows, rows), rows), columns], gqo),
        (gk.at[0, :, columns], gk.at[0, :, columns], gko),
        (gv.at[0, :, columns], gv.at[0, :, columns], gvo),
        (rb.at[0], rb.at[0], rbo),
    )

    @pl.when(owner == c)
    def _():
        for n, (own, other, dst) in enumerate(shared):
            pltpu.make_async_copy(own, dst, c_recv.at[n]).start()
            remote(other, dst, c_send.at[n], c_recv.at[n], sibling, s).start()

    send(2)
    send(3)

    width = fo.shape[2]

    def send_f(i, carry):
        to_x, to_y = (x + i // NY) % xs, (y + i) % NY
        src = f.at[0, :, pl.ds(pl.multiple_of(to_x * width, width), width)]
        remote(src, fo.at[x * NY + y], f_send, f_recv, to_x * NC + c, z * NY + to_y).start()
        return carry

    src = f.at[0, :, pl.ds(pl.multiple_of(x * width, width), width)]
    pltpu.make_async_copy(src, fo.at[x * NY + y], f_recv).start()
    lax.fori_loop(1, xs * NY, send_f, 0)

    def arrived(ref, sem):
        pltpu.make_async_copy(ref, ref, sem).wait()

    part = pl.ds(pl.multiple_of(c * half, half), half)
    other_part = pl.ds(pl.multiple_of((1 - c) * half, half), half)
    for n, out in enumerate((ko, vo)):
        arrived(out.at[part], a_recv.at[n])
        remote(out.at[part], out.at[part], b_send.at[n], b_recv.at[n], sibling, s).start()
    arrived(qo, a_recv.at[2])
    arrived(go, a_recv.at[3])
    for n, out in enumerate((ko, vo)):
        arrived(out.at[other_part], b_recv.at[n])
    for n, (_, _, dst) in enumerate(shared):
        arrived(dst, c_recv.at[n])
    arrived(fo, f_recv)

    for n in range(4):
        @pl.when(mine)
        def _():
            arrived(qo.at[pl.ds(0, half - 1)], a_send.at[n])

        @pl.when(jnp.logical_not(mine))
        def _():
            arrived(qo, a_send.at[n])
    for n, out in enumerate((ko, vo)):
        arrived(out.at[part], b_send.at[n])

    @pl.when(owner == c)
    def _():
        for n, (_, _, dst) in enumerate(shared):
            arrived(dst, c_send.at[n])

    arrived(fo.at[pl.ds(0, xs * NY - 1)], f_send)


def shuffle(seqs, xs, q, k, v, g, f, gq, gk, gv, rb):
    tokens, wide = q.shape[1], f.shape[2]
    half = seqs // 2
    bf16 = jnp.bfloat16
    shape = jax.ShapeDtypeStruct
    outs = (
        shape((half, tokens, E), bf16),
        shape((seqs, tokens, E), bf16),
        shape((seqs, tokens, E), bf16),
        shape((half, tokens, E), bf16),
        shape((xs * NY, tokens, wide // xs), bf16),
        shape((gq.shape[1] // NC, E), bf16),
        shape((gk.shape[1], E), bf16),
        shape((gv.shape[1], E), bf16),
        shape(rb.shape[1:], jnp.int32),
    )
    dma = pltpu.SemaphoreType.DMA
    return pl.pallas_call(
        functools.partial(shuffle_kernel, seqs, xs),
        out_shape=outs,
        in_specs=[ANY] * 9,
        out_specs=[ANY] * 9,
        scratch_shapes=[dma((4,)), dma((4,)), dma((2,)), dma((2,)), dma, dma, dma((4,)), dma((4,))],
        compiler_params=pltpu.CompilerParams(collective_id=0, has_side_effects=True),
        name="shuffle",
    )(q, k, v, g, f, gq, gk, gv, rb)


def attention_kernel(blocks, rb, q, k, v, g, gq, gk, gv, att, grad, gatt):
    scaling = 1.0 / math.sqrt(E)
    count = q.shape[0] // BLOCK
    c = lax.axis_index("dp") % NC
    dot = functools.partial(lax.dot_general, preferred_element_type=jnp.float32)
    nt = (((1,), (1,)), ((), ()))
    nn = (((1,), (0,)), ((), ()))
    g_k, g_v = gk[...], gv[...]
    columns = 3 * BLOCK + R * BLOCK + g_k.shape[0]

    def rows(b):
        return pl.ds(pl.multiple_of(b * BLOCK, BLOCK), BLOCK)

    def block(i, carry):
        b = c * count + i
        first = jnp.clip(b - 1, 0, blocks - 3)
        window = pl.ds(pl.multiple_of(first * BLOCK, BLOCK), 3 * BLOCK)
        picks = [rows(rb[b, n]) for n in range(R)]
        keys = jnp.concatenate([k[window, :]] + [k[p, :] for p in picks] + [g_k], axis=0)
        values = jnp.concatenate([v[window, :]] + [v[p, :] for p in picks] + [g_v], axis=0)
        q_b, g_b = q[rows(i), :], g[rows(i), :]
        scores = dot(q_b, keys, nt) * scaling
        low = jnp.where(b == blocks - 1, BLOCK, 0)
        high = jnp.where(b == 0, 2 * BLOCK, 3 * BLOCK)
        column = lax.broadcasted_iota(jnp.int32, (BLOCK, columns), 1)
        valid = (column >= low) & ((column < high) | (column >= 3 * BLOCK))
        scores = jnp.where(valid, scores, NEGATIVE)
        peak = jnp.max(scores, axis=-1, keepdims=True)
        weights = jnp.exp(scores - peak)
        probs = weights / jnp.sum(weights, axis=-1, keepdims=True)
        attended = dot(probs.astype(jnp.bfloat16), values, nn).astype(jnp.bfloat16)
        delta = jnp.sum(
            g_b.astype(jnp.float32) * attended.astype(jnp.float32), axis=-1, keepdims=True
        )
        dprobs = dot(g_b, values, nt)
        dscores = (probs * (dprobs - delta)).astype(jnp.bfloat16)
        att[rows(i), :] = attended
        grad[rows(i), :] = (dot(dscores, keys, nn) * scaling).astype(jnp.bfloat16)
        return carry

    lax.fori_loop(0, count, block, 0, unroll=2)

    g_q = gq[...]
    long_scores = dot(g_q, k[...], nt) * scaling
    own_scores = dot(g_q, g_k, nt) * scaling
    peak = jnp.maximum(
        jnp.max(long_scores, axis=-1, keepdims=True), jnp.max(own_scores, axis=-1, keepdims=True)
    )
    long_weights = jnp.exp(long_scores - peak)
    own_weights = jnp.exp(own_scores - peak)
    mass = jnp.sum(long_weights, axis=-1, keepdims=True) + jnp.sum(own_weights, axis=-1, keepdims=True)
    total = dot(long_weights.astype(jnp.bfloat16), v[...], nn)
    total = total + dot(own_weights.astype(jnp.bfloat16), g_v, nn)
    gatt[...] = (total / mass).astype(jnp.bfloat16)


def attention(q, k, v, g, gq, gk, gv, rb):
    flat = [a.reshape(-1, E) for a in (q, k, v, g)]
    shape = jax.ShapeDtypeStruct
    vmem = pl.BlockSpec(memory_space=pltpu.VMEM)
    return pl.pallas_call(
        functools.partial(attention_kernel, flat[1].shape[0] // BLOCK),
        out_shape=(
            shape(flat[0].shape, jnp.bfloat16),
            shape(flat[0].shape, jnp.bfloat16),
            shape(gq.shape, jnp.bfloat16),
        ),
        in_specs=[pl.BlockSpec(memory_space=pltpu.SMEM)] + [vmem] * 7,
        out_specs=[vmem] * 3,
        compiler_params=pltpu.CompilerParams(vmem_limit_bytes=40 << 20),
        name="attention",
    )(rb, *flat, gq, gk, gv)


def product_kernel(seqs, xs, *refs):
    att, grad, gatt, f = refs[:4]
    att_o, gatt_o, w_o = refs[4:7]
    (f_v, grads, total, from_sibling, part, pieces,
     o_send, o_recv, g_send, g_recv, n_send, n_recv, x_send, x_recv,
     s_send, s_recv, w_send, w_recv, f_sem) = refs[7:]
    d, s, x, c, z, y = place(seqs)
    half = seqs // 2
    tokens = att_o.shape[0]
    owner = z % NC
    sibling = x * NC + (1 - c)
    doc = x * NC + owner
    head = (z // NC) * NY + y
    rows_z = half // NY
    mine = jnp.logical_and(owner == c, z // rows_z == c)

    load = pltpu.make_async_copy(f, f_v, f_sem)
    load.start()

    barrier = pltpu.get_barrier_semaphore()

    def greet(i, carry):
        from_z = (i // NY) * NC + c
        from_s = from_z * NY + i % NY
        for t in range(NC):
            @pl.when(jnp.logical_not(jnp.logical_and(from_s == s, c == t)))
            def _():
                signal(barrier, x * NC + t, from_s)

        return carry

    lax.fori_loop(0, half, greet, 0)
    signal(barrier, sibling, s)
    lax.fori_loop(1, xs, lambda i, a: (signal(barrier, ((x + i) % xs) * NC + c, s), a)[1], 0)
    lax.fori_loop(1, seqs, lambda i, a: (signal(barrier, d, (s + i) % seqs), a)[1], 0)

    @pl.when(owner == c)
    def _():
        pl.semaphore_wait(barrier, 2 * seqs - 1 + xs - 1)

    @pl.when(owner != c)
    def _():
        pl.semaphore_wait(barrier, 2 * seqs + xs - 1)

    columns = head_columns(head)

    span = NY * tokens
    my_columns = head_columns(y)

    def send_g(i, carry):
        r = (i + s) % rows_z
        to = (c * rows_z + r) * NY + z // NC
        src = grad.at[pl.ds(pl.multiple_of(r * span, span), span), :]
        dst = grads.at[x, :, my_columns]
        here = jnp.logical_and(owner == c, to == s)

        @pl.when(here)
        def _():
            pltpu.make_async_copy(src, dst, g_recv).start()

        @pl.when(jnp.logical_not(here))
        def _():
            remote(src, dst, g_send, g_recv, doc, to).start()

        return carry

    lax.fori_loop(0, rows_z, send_g, 0)

    def send_o(i, carry):
        r = (i + s) % half
        to = c * half + r
        src = att.at[pl.ds(pl.multiple_of(r * tokens, tokens), tokens), :]
        dst = att_o.at[:, columns]
        here = jnp.logical_and(owner == c, to == s)

        @pl.when(here)
        def _():
            pltpu.make_async_copy(src, dst, o_recv).start()

        @pl.when(jnp.logical_not(here))
        def _():
            remote(src, dst, o_send, o_recv, doc, to).start()

        return carry

    lax.fori_loop(0, half, send_o, 0)

    g_rows = gatt.shape[0]
    g_dst = gatt_o.at[pl.ds(pl.multiple_of(c * g_rows, g_rows), g_rows), columns]

    def send_n(i, carry):
        to = (i + s) % seqs
        here = jnp.logical_and(owner == c, i == 0)

        @pl.when(here)
        def _():
            pltpu.make_async_copy(gatt, g_dst, n_recv).start()

        @pl.when(jnp.logical_not(here))
        def _():
            remote(gatt, g_dst, n_send, n_recv, doc, to).start()

        return carry

    lax.fori_loop(0, seqs, send_n, 0)

    def arrived(ref, sem):
        pltpu.make_async_copy(ref, ref, sem).wait()

    arrived(grads.at[x], g_recv)
    for i in range(1, xs):
        to = (x + i) % xs
        remote(grads.at[x], grads.at[x], x_send.at[i - 1], x_recv.at[i - 1], to * NC + c, s).start()
    load.wait()
    depth = NY * tokens

    def product(source):
        lhs = f_v[pl.ds(pl.multiple_of(source * depth, depth), depth), :]
        return lax.dot_general(
            lhs, grads[source], (((0,), (0,)), ((), ())), preferred_element_type=jnp.float32
        )

    total[...] = product(x)
    for i in (1, xs - 1, *range(2, xs - 1)):
        if i >= xs or (i == xs - 1 and i == 1 and xs != 2):
            continue
        source = (x - i + xs) % xs
        arrived(grads.at[source], x_recv.at[i - 1])
        total[...] += product(source)
        if xs == 2:
            break

    rows = part.shape[0]
    other = total.at[pl.ds(pl.multiple_of((1 - c) * rows, rows), rows), :]
    remote(other, from_sibling, s_send, s_recv, sibling, s).start()
    arrived(from_sibling, s_recv)
    part[...] = total[pl.ds(pl.multiple_of(c * rows, rows), rows), :] + from_sibling[...]

    out_rows = w_o.shape[0]

    def send_w(i, carry):
        to = (i + s) % seqs
        src = part.at[pl.ds(pl.multiple_of(to * out_rows, out_rows), out_rows), :]
        remote(src, pieces.at[s], w_send, w_recv, d, to).start()
        return carry

    src = part.at[pl.ds(pl.multiple_of(s * out_rows, out_rows), out_rows), :]
    pltpu.make_async_copy(src, pieces.at[s], w_recv).start()
    lax.fori_loop(1, seqs, send_w, 0)
    arrived(pieces, w_recv)
    group = part.shape[1]
    for n in range(NY):
        acc = pieces[n]
        for m in range(1, seqs // NY):
            acc = acc + pieces[m * NY + n]
        w_o[:, n * group : (n + 1) * group] = acc

    arrived(att_o, o_recv)
    arrived(gatt_o, n_recv)

    @pl.when(mine)
    def _():
        arrived(att.at[pl.ds(0, (half - 1) * tokens), :], o_send)

    @pl.when(jnp.logical_not(mine))
    def _():
        arrived(att, o_send)

    mine_g = jnp.logical_and(mine, y == z // NC)

    @pl.when(mine_g)
    def _():
        arrived(grad.at[pl.ds(0, (rows_z - 1) * span), :], g_send)

    @pl.when(jnp.logical_not(mine_g))
    def _():
        arrived(grad, g_send)

    stand_in = gatt_o.at[pl.ds(0, g_rows), :]

    @pl.when(owner == c)
    def _():
        whole = att_o.shape[1] // E
        arrived(stand_in, n_send)
        arrived(gatt_o.at[pl.ds(0, g_rows), pl.ds(0, (whole - 1) * E)], n_send)

    @pl.when(owner != c)
    def _():
        arrived(gatt_o, n_send)

    for i in range(1, xs):
        arrived(grads.at[x], x_send.at[i - 1])
    arrived(from_sibling, s_send)
    arrived(pieces.at[pl.ds(0, seqs - 1)], w_send)


def product(seqs, xs, att, grad, gatt, f, wide, rows):
    tokens = att.shape[0] // (seqs // 2)
    hd = (seqs // 2) * E
    group = hd // NY
    shape = jax.ShapeDtypeStruct
    dma = pltpu.SemaphoreType.DMA
    f = f.reshape(-1, f.shape[2])
    return pl.pallas_call(
        functools.partial(product_kernel, seqs, xs),
        out_shape=(
            shape((tokens, hd), jnp.bfloat16),
            shape((gatt.shape[0] * NC, hd), jnp.bfloat16),
            shape((rows, hd), jnp.float32),
        ),
        in_specs=[ANY] * 4,
        out_specs=[ANY, ANY, pl.BlockSpec(memory_space=pltpu.VMEM)],
        scratch_shapes=[
            pltpu.VMEM(f.shape, jnp.bfloat16),
            pltpu.VMEM((xs, NY * tokens, group), jnp.bfloat16),
            pltpu.VMEM((wide // xs, group), jnp.float32),
            pltpu.VMEM((wide // xs // NC, group), jnp.float32),
            pltpu.VMEM((wide // xs // NC, group), jnp.float32),
            pltpu.VMEM((seqs, rows, group), jnp.float32),
            dma, dma, dma, dma, dma, dma, dma((xs - 1,)), dma((xs - 1,)),
            dma, dma, dma, dma, dma,
        ],
        compiler_params=pltpu.CompilerParams(
            collective_id=1, has_side_effects=True, vmem_limit_bytes=40 << 20
        ),
        name="product",
    )(att, grad, gatt, f)


def per_device(seqs, xs, features, queries, key_rows, value_rows, cotangent,
               global_queries, global_keys, global_values, random_blocks):
    wide = features.shape[2]
    q, k, v, g, f, gq, gk, gv, rb = shuffle(
        seqs, xs, queries, key_rows, value_rows, cotangent, features,
        global_queries, global_keys, global_values, random_blocks,
    )
    att, grad, gatt = attention(q, k, v, g, gq, gk, gv, rb)
    rows = wide // (seqs * xs * NC)
    attended, global_attended, weight_grad = product(seqs, xs, att, grad, gatt, f, wide, rows)
    return attended[None], global_attended[None], weight_grad


def solution(mesh):
    seqs, xs = mesh.shape["seq"], mesh.shape["dp"] // NC
    long, whole = P("dp", "seq", None), P("dp", None, None)
    return jax.shard_map(
        functools.partial(per_device, seqs, xs),
        mesh=mesh,
        in_specs=(long,) * 5 + (whole,) * 4,
        out_specs=(long, whole, P(("dp", "seq"), None)),
        check_vma=False,
    )
```

time: 888 us -> 168 us (0.19)
  waiting for transfers between devices: 594 us -> 0 us
  Pallas kernels: 0 us -> 156 us
  blocking collectives: 100 us -> 0 us
  local copies, waits for them, and re-layouts: 95.9 us -> 11.1 us
  other arithmetic: 33.2 us -> 0 us
  matrix products: 25 us -> 0 us
  starting transfers between devices: 17.5 us -> 0 us
  between operations: 14.3 us -> 0.68 us
    all_to_all x1 -> x0, waiting for transfers between devices: 370 us -> none  [per_device(): lax.all_to_all(outgoing, 'seq', split_axis=0, concat_axis=0, tiled=True)]
    unnamed x5 -> x0, waiting for transfers between devices: 160 us -> none
    pallas_call x0 -> x3, Pallas kernels: none -> 156 us  [the longest x1 73.3 us: product(): pl.pallas_call(functools.partial(product_kernel, seqs, xs), out_shape=(sh...]
    all_gather x2 -> x0, blocking collectives: 100 us -> none  [merged_2(): gathered = jax.tree.map(lambda a: lax.all_gather(a, axis), part)]
    ppermute x2 -> x0, waiting for transfers between devices: 64 us -> none  [the longest x1 43.6 us: padded_2(): before = lax.ppermute(last, axis, up)]
    dynamic_slice x34 -> x0, local copies, waits for them, and re-layouts: 34.9 us -> none  [take(): lax.dynamic_index_in_dim(a, source, 0, False)]
    dot_general x16 -> x0, matrix products: 23.7 us -> none  [the longest x1 8.09 us: per_device(): lax.dot_general(permuted, query_grad, (((0,), (0,)), ((), ())), preferred...]
    unnamed x69 -> x22, local copies, waits for them, and re-layouts: 30 us -> 11.1 us
  transfers between devices with their start and end apart: 6 -> 0, of which waited for: 4 -> 0; matrix products, arithmetic and copies ran while one was open for 16% -> 0% of each run, Pallas kernels for 0% -> 0%
where the time goes in v1:
time: 168 us
  Pallas kernels  156 us (93%)
  local copies, waits for them, and re-layouts  11.1 us (7%)
    pallas_call x1, Pallas kernels, product(): pl.pallas_call(functools.partial(product_kernel, seqs, xs), out_shape=(sh...  73.3 us
    pallas_call x1, Pallas kernels, shuffle(): pl.pallas_call(functools.partial(shuffle_kernel, seqs, xs), out_shape=out...  59.1 us
    pallas_call x1, Pallas kernels, attention(): pl.pallas_call(functools.partial(attention_kernel, flat[1].shape[0] // BL...  23.6 us
    unnamed x22, local copies, waits for them, and re-layouts  11.1 us

profile of v1, /device:TPU:1, one launch (start us, length us, event | category | flops | bytes accessed | tf_op | source)
XLA Modules:
  0.0 167.7 jit_solution(18155603330883197360)
XLA Ops:
  0.6 1.4 copy.12.refs_8_
  2.0 59.1 %shuffle.1 = (bf16[16,128,128]{2,1,0:T(8,128)(2,1)}, bf16[32,128,128]{2,1,0:T(8,128)(2,1)}, bf16[32,128,128]{2,1,0:T(8,128)(2,1)}, bf16[16,128,128]{2,1,0:T(8,12...) custom-call(bf16[1,128,2048]{2,1,0:T(8,128)(2,1)} %refs_0_.1, ...), custom_call_target="tpu_custom_call" | custom-call | tf_op jit(solution)/shard_map/shuffle/pallas_call | solution.py:200
  61.2 0.0 copy-start
  61.2 0.0 copy-start.1
  61.2 1.4 copy-done.1
  62.5 0.0 copy-start.2
  62.6 1.2 copy-done.2
  63.8 0.0 copy-start.3
  63.8 1.0 copy-done.3
  64.8 0.0 copy-start.4
  64.8 1.0 copy-done.4
  65.9 0.0 copy-start.5
  65.9 0.8 copy-done.5
  66.6 0.0 copy-start.6
  66.6 0.7 copy-done.6
  67.3 0.0 copy-start.7
  67.3 0.7 copy-done.7
  68.1 0.0 copy-start.8
  68.1 0.7 copy-done.8
  68.8 23.6 %attention.1 = (bf16[2048,128]{1,0:T(8,128)(2,1)S(1)}, bf16[2048,128]{1,0:T(8,128)(2,1)S(1)}, bf16[32,128]{1,0:T(8,128)(2,1)S(1)}) custom-call(s32[64,3]{1,0:T(8,128)S(1)} %copy-done.5, bf16[2048,128]{1,0:T(8,128)(2,1)S(1)} %bitcast.10, bf16[4096,128]{1,0:T(8,128)(2,1)S(1)} %bitcast.8, bf16[4096,128]{1,0:T(8,128)(2,1)S(1)} %bitcast.9, ...), custom_call_target="tpu_custom_call" | custom-call | tf_op jit(solution)/shard_map/attention/pallas_call | solution.py:271
  92.3 0.0 copy-done
  92.3 73.3 %product.1 = (bf16[128,2048]{1,0:T(8,128)(2,1)S(1)}, bf16[64,2048]{1,0:T(8,128)(2,1)S(1)}, f32[8,2048]{1,0:T(8,128)S(1)}) custom-call(bf16[2048,128]{1,0:T(8,128)(2,1)S(1)} %get-tuple-element.26.refs_0_, bf16[2048,128]{1,0:T(8,128)(2,1)S(1)} %get-tuple-element.27.refs_1_, bf16[32,128]{1,0:T(8,128)(2,1)S(1)} %get-tuple-element.28.refs_2_, ...), custom_call_target="tpu_custom_call" | custom-call | tf_op jit(solution)/shard_map/product/pallas_call | solution.py:488
  165.6 0.8 copy.16
  166.4 0.7 copy.17
  167.1 0.6 copy.18
Async XLA Ops:
  61.2 31.2 %copy-start = (bf16[16,128,512]{2,1,0:T(8,128)(2,1)S(1)}, bf16[16,128,512]{2,1,0:T(8,128)(2,1)}, u32[]{:S(2)}) copy-start(bf16[16,128,512]{2,1,0:T(8,128)(2,1)} %get-tuple-element.29) | copy-start | bytes 6291460
  61.2 1.4 copy-start.1
  62.5 1.2 copy-start.2
  63.8 1.0 copy-start.3
  64.8 1.0 copy-start.4
  65.9 0.8 copy-start.5
  66.6 0.7 copy-start.6
  67.3 0.7 copy-start.7
  68.1 0.7 copy-start.8

commit v2 on v1

v2 whole, which is shorter than its diff:
```python
import functools
import math

import jax
import jax.numpy as jnp
from jax import lax
from jax.experimental import pallas as pl
from jax.experimental.pallas import tpu as pltpu
from jax.sharding import PartitionSpec as P

E = 128
BLOCK = 64
R = 3
NY = 4
NC = 2
NEGATIVE = -1e30
MESH = pl.DeviceIdType.MESH
ANY = pl.BlockSpec(memory_space=pl.ANY)


def place(seqs):
    d, s = lax.axis_index("dp"), lax.axis_index("seq")
    return d, s, d // NC, d % NC, s // NY, s % NY


def head_columns(h):
    return pl.ds(pl.multiple_of(h * E, E), E)


def remote(src, dst, send, recv, d, s):
    return pltpu.make_async_remote_copy(
        src_ref=src, dst_ref=dst, send_sem=send, recv_sem=recv, device_id=(d, s), device_id_type=MESH
    )


def signal(sem, d, s):
    pl.semaphore_signal(sem, inc=1, device_id=(d, s), device_id_type=MESH)


def arrived(ref, sem):
    pltpu.make_async_copy(ref, ref, sem).wait()


def span(i, size):
    return pl.ds(pl.multiple_of(i * size, size), size)


def flip(a, i):
    low = (a % 2 + i % 2) % 2
    high = (a // 2 + i // 2) % max(NY // 2, 1)
    return high * 2 + low


dot = functools.partial(lax.dot_general, preferred_element_type=jnp.float32)
NT = (((1,), (1,)), ((), ()))
NN = (((1,), (0,)), ((), ()))


def layer_kernel(seqs, xs, *refs):
    q, k, v, g, f, gq, gk, gv, rb = refs[:9]
    att_o, gatt_o, w_o = refs[9:12]
    (qs, ks, vs, gs, fs, gqs, gks, gvs, rbv, rbs,
     probs, long_weights, own_weights, mass, att, grad, gatt, grads, turned,
     total, sib_out, sib_in, part, pieces,
     a_send, a_recv, b_send, b_recv, f_send, f_recv, c_send, c_recv, r_sem,
     o_send, o_recv, g_send, g_recv, n_send, n_recv, x_send, x_recv,
     s_send, s_recv, w_send, w_recv) = refs[12:]
    d, s, x, c, z, y = place(seqs)
    half = seqs // 2
    heads = half
    rows_z = half // NY
    tokens = att_o.shape[0]
    side = s // half
    slot = s % half
    sibling = x * NC + (1 - c)
    owner = z % NC
    doc = x * NC + owner
    head = (z // NC) * NY + y
    mine = jnp.logical_and(owner == c, side == c)
    others = jnp.logical_not(mine)
    scaling = 1.0 / math.sqrt(E)

    barrier = pltpu.get_barrier_semaphore()

    def greet(i, carry):
        source = c * half + i

        @pl.when(jnp.logical_not(jnp.logical_and(owner == c, source == s)))
        def _():
            signal(barrier, doc, source)

        return carry

    lax.fori_loop(0, half, greet, 0)
    signal(barrier, sibling, s)

    def greet_f(i, carry):
        signal(barrier, ((x + i // NY) % xs) * NC + c, z * NY + (y + i) % NY)
        return carry

    lax.fori_loop(1, xs * NY, greet_f, 0)

    @pl.when(mine)
    def _():
        pl.semaphore_wait(barrier, half + xs * NY - 1)

    @pl.when(others)
    def _():
        pl.semaphore_wait(barrier, half + xs * NY)

    def spread(n, array, dst):
        def body(i, carry):
            h = (i + s) % heads
            to = ((h // NY) * NC + c) * NY + h % NY
            src = array.at[..., head_columns(h)]
            here = jnp.logical_and(mine, to == s)

            @pl.when(here)
            def _():
                pltpu.make_async_copy(src, dst, a_recv.at[n]).start()

            @pl.when(jnp.logical_not(here))
            def _():
                remote(src, dst, a_send.at[n], a_recv.at[n], x * NC + side, to).start()

            return carry

        lax.fori_loop(0, heads, body, 0)

    g_rows = gqs.shape[0]
    columns = head_columns(head)
    shared = (
        (gq.at[0, span(c, g_rows), columns], gq.at[0, span(1 - c, g_rows), columns], gqs),
        (gk.at[0, :, columns], gk.at[0, :, columns], gks),
        (gv.at[0, :, columns], gv.at[0, :, columns], gvs),
        (rb, rb, rbv),
    )

    own_blocks = tokens // BLOCK

    spread(0, k, ks.at[span(s, own_blocks)])
    spread(2, q, qs.at[span(slot, tokens), :])

    @pl.when(owner == c)
    def _():
        for n, (own, other, dst) in enumerate(shared):
            pltpu.make_async_copy(own, dst, c_recv.at[n]).start()
            remote(other, dst, c_send.at[n], c_recv.at[n], sibling, s).start()

    spread(1, v, vs.at[span(s, own_blocks)])
    spread(3, g, gs.at[span(slot, tokens), :])

    width = fs.shape[1]
    f_dst = fs.at[span(x * NY + y, tokens), :]

    def send_f(i, carry):
        to_x, to_y = (x + i // NY) % xs, (y + i) % NY
        src = f.at[0, :, span(to_x, width)]
        remote(src, f_dst, f_send, f_recv, to_x * NC + c, z * NY + to_y).start()
        return carry

    pltpu.make_async_copy(f.at[0, :, span(x, width)], f_dst, f_recv).start()
    lax.fori_loop(1, xs * NY, send_f, 0)

    for n, (_, _, dst) in enumerate(shared):
        arrived(dst, c_recv.at[n])
    pltpu.make_async_copy(rbv, rbs, r_sem).start()
    pltpu.make_async_copy(rbv, rbs, r_sem).wait()

    blocks = ks.shape[0]
    count = blocks // 2
    own_part, other_part = span(c, count), span(1 - c, count)

    def share(n, ref):
        arrived(ref.at[own_part], a_recv.at[n])
        remote(ref.at[own_part], ref.at[own_part], b_send.at[n], b_recv.at[n], sibling, s).start()

    share(0, ks)
    arrived(qs, a_recv.at[2])
    arrived(ks.at[other_part], b_recv.at[0])

    g_k, g_v = gks[...], gvs[...]
    width_k = probs.shape[1]

    def listed(ref, b, own):
        first = jnp.clip(b - 1, 0, blocks - 3)
        window = [ref[first + n] for n in range(3)]
        picks = [ref[rbs[n, 0, b]] for n in range(R)]
        return jnp.concatenate(window + picks + [own], axis=0)

    def forward(i, carry):
        b = c * count + i
        scores = dot(qs[span(i, BLOCK), :], listed(ks, b, g_k), NT) * scaling
        low = jnp.where(b == blocks - 1, BLOCK, 0)
        high = jnp.where(b == 0, 2 * BLOCK, 3 * BLOCK)
        column = lax.broadcasted_iota(jnp.int32, (BLOCK, width_k), 1)
        valid = (column >= low) & ((column < high) | (column >= 3 * BLOCK))
        scores = jnp.where(valid, scores, NEGATIVE)
        weights = jnp.exp(scores - jnp.max(scores, axis=-1, keepdims=True))
        probs[span(i, BLOCK), :] = weights / jnp.sum(weights, axis=-1, keepdims=True)
        return carry

    lax.fori_loop(0, count, forward, 0, unroll=4)

    g_q = gqs[...]
    long_scores = dot(g_q, ks[...].reshape(-1, E), NT) * scaling
    own_scores = dot(g_q, g_k, NT) * scaling
    peak = jnp.maximum(
        jnp.max(long_scores, axis=-1, keepdims=True), jnp.max(own_scores, axis=-1, keepdims=True)
    )
    long_scores = jnp.exp(long_scores - peak)
    own_scores = jnp.exp(own_scores - peak)
    mass[...] = jnp.sum(long_scores, axis=-1, keepdims=True) + jnp.sum(
        own_scores, axis=-1, keepdims=True
    )
    long_weights[...] = long_scores.astype(jnp.bfloat16)
    own_weights[...] = own_scores.astype(jnp.bfloat16)

    share(1, vs)
    arrived(gs, a_recv.at[3])
    arrived(vs.at[other_part], b_recv.at[1])

    per_chunk = count // NY
    deep = NY * tokens
    my_row = z % rows_z

    def backward(i, carry):
        b = c * count + i
        rows = span(i, BLOCK)
        values = listed(vs, b, g_v)
        p = probs[rows, :]
        g_b = gs[rows, :]
        attended = dot(p.astype(jnp.bfloat16), values, NN).astype(jnp.bfloat16)
        delta = jnp.sum(
            g_b.astype(jnp.float32) * attended.astype(jnp.float32), axis=-1, keepdims=True
        )
        dprobs = dot(g_b, values, NT)
        dscores = (p * (dprobs - delta)).astype(jnp.bfloat16)
        att[rows, :] = attended
        grad[rows, :] = (dot(dscores, listed(ks, b, g_k), NN) * scaling).astype(jnp.bfloat16)
        return carry

    def send_g(i):
        r = flip(y, i)
        to = (c * rows_z + r) * NY + z // NC
        src, dst = grad.at[span(r, deep), :], grads.at[x, i]
        here = jnp.logical_and(owner == c, to == s)

        @pl.when(here)
        def _():
            pltpu.make_async_copy(src, dst, g_recv.at[i]).start()

        @pl.when(jnp.logical_not(here))
        def _():
            remote(src, dst, g_send.at[i], g_recv.at[i], doc, to).start()

    def pass_on(i):
        arrived(grads.at[x, i], g_recv.at[i])
        for j in range(1, xs):
            remote(
                grads.at[x, i], grads.at[x, i], x_send.at[i, j - 1], x_recv.at[i, j - 1],
                ((x + j) % xs) * NC + c, s,
            ).start()

    for i in range(NY):
        first = flip(y, i) * per_chunk
        lax.fori_loop(
            0, per_chunk, lambda n, a, first=first: backward(first + n, a), 0, unroll=4
        )
        send_g(i)
        if i > 0:
            pass_on(i - 1)

    def send_o(i, carry):
        r = (i + s) % half
        to = c * half + r
        src, dst = att.at[span(r, tokens), :], att_o.at[:, columns]
        here = jnp.logical_and(owner == c, to == s)

        @pl.when(here)
        def _():
            pltpu.make_async_copy(src, dst, o_recv).start()

        @pl.when(jnp.logical_not(here))
        def _():
            remote(src, dst, o_send, o_recv, doc, to).start()

        return carry

    lax.fori_loop(0, half, send_o, 0)

    sums = dot(long_weights[...], vs[...].reshape(-1, E), NN) + dot(own_weights[...], g_v, NN)
    gatt[...] = (sums / mass[...]).astype(jnp.bfloat16)

    pass_on(NY - 1)

    g_dst = gatt_o.at[span(c, g_rows), columns]

    def send_n(i, carry):
        to = (i + s) % seqs
        here = jnp.logical_and(owner == c, i == 0)

        @pl.when(here)
        def _():
            pltpu.make_async_copy(gatt, g_dst, n_recv).start()

        @pl.when(jnp.logical_not(here))
        def _():
            remote(gatt, g_dst, n_send, n_recv, doc, to).start()

        return carry

    lax.fori_loop(0, seqs, send_n, 0)

    arrived(fs, f_recv)
    for i in range(xs):
        turned[i] = fs[i * deep : (i + 1) * deep, :].T

    pairs = NY // 2
    pair = 2 * E
    rows = sib_in.shape[1]
    bit = my_row % 2
    for p in range(pairs):
        for i in (2 * p, 2 * p + 1):
            for j in range(1, xs):
                arrived(grads.at[(x + xs - j) % xs, i], x_recv.at[i, j - 1])
        acc = None
        for source in range(xs):
            rhs = jnp.concatenate(
                [grads[source, 2 * p + bit], grads[source, 2 * p + 1 - bit]], axis=1
            )
            term = dot(turned[source], rhs, NN)
            acc = term if acc is None else acc + term
        total[p] = acc
        sib_out[p] = total[p, span(1 - c, rows), :].astype(jnp.bfloat16)
        remote(sib_out.at[p], sib_in.at[p], s_send.at[p], s_recv.at[p], sibling, s).start()

    out_rows = w_o.shape[0]
    for p in range(pairs):
        arrived(sib_in.at[p], s_recv.at[p])
        block = total[p, span(c, rows), :] + sib_in[p].astype(jnp.float32)
        part[p] = block.astype(jnp.bfloat16).reshape(seqs, out_rows, pair)
        place_p = (my_row // 2 + p) % pairs
        dst = pieces.at[place_p, s]
        pltpu.make_async_copy(part.at[p, s], dst, w_recv).start()

        def send_w(i, carry, p=p, dst=dst):
            to = (i + s) % seqs
            remote(part.at[p, to], dst, w_send, w_recv, d, to).start()
            return carry

        lax.fori_loop(1, seqs, send_w, 0)

    arrived(pieces, w_recv)
    for n in range(NY):
        for p in range(pairs):
            acc = pieces[p, n].astype(jnp.float32)
            for m in range(1, seqs // NY):
                acc = acc + pieces[p, m * NY + n].astype(jnp.float32)
            start = (n * pairs + p) * pair
            w_o[:, start : start + pair] = acc

    arrived(att_o, o_recv)
    arrived(gatt_o, n_recv)

    for n in range(4):
        @pl.when(mine)
        def _():
            arrived(qs.at[pl.ds(0, (half - 1) * tokens), :], a_send.at[n])

        @pl.when(others)
        def _():
            arrived(qs, a_send.at[n])
    for n, ref in enumerate((ks, vs)):
        arrived(ref.at[own_part], b_send.at[n])

    @pl.when(owner == c)
    def _():
        for n, (_, _, dst) in enumerate(shared):
            arrived(dst, c_send.at[n])

    arrived(fs.at[pl.ds(0, (xs * NY - 1) * tokens), :], f_send)

    for i in range(NY):
        to = (c * rows_z + flip(y, i)) * NY + z // NC

        @pl.when(jnp.logical_not(jnp.logical_and(owner == c, to == s)))
        def _():
            arrived(grads.at[x, i], g_send.at[i])

        for j in range(1, xs):
            arrived(grads.at[x, i], x_send.at[i, j - 1])

    @pl.when(mine)
    def _():
        arrived(att.at[pl.ds(0, (half - 1) * tokens), :], o_send)

    @pl.when(others)
    def _():
        arrived(att, o_send)

    @pl.when(owner == c)
    def _():
        arrived(att.at[pl.ds(0, (seqs - 1) * g_rows), :], n_send)

    @pl.when(owner != c)
    def _():
        arrived(att.at[pl.ds(0, seqs * g_rows), :], n_send)

    for p in range(pairs):
        arrived(sib_in.at[p], s_send.at[p])
    arrived(pieces.at[:, pl.ds(0, seqs - 1)], w_send)


def layer(seqs, xs, q, k, v, g, f, gq, gk, gv, rb):
    tokens, hd, wide = q.shape[1], q.shape[2], f.shape[2]
    half, globals_ = seqs // 2, gk.shape[1]
    rows = wide // (seqs * xs * NC)
    width, g_rows, pair = wide // xs, globals_ // NC, 2 * E
    pairs, deep, length = NY // 2, NY * tokens, seqs * tokens
    columns = 3 * BLOCK + R * BLOCK + globals_
    shape, vmem, dma = jax.ShapeDtypeStruct, pltpu.VMEM, pltpu.SemaphoreType.DMA
    bf16, f32 = jnp.bfloat16, jnp.float32
    rb = jnp.transpose(rb, (2, 0, 1))
    q, g = q[0], g[0]
    k, v = (a.reshape(-1, BLOCK, hd) for a in (k, v))
    return pl.pallas_call(
        functools.partial(layer_kernel, seqs, xs),
        out_shape=(
            shape((tokens, hd), bf16),
            shape((globals_, hd), bf16),
            shape((rows, hd), f32),
        ),
        in_specs=[ANY] * 9,
        out_specs=[ANY, ANY, pl.BlockSpec(memory_space=vmem)],
        scratch_shapes=[
            vmem((half * tokens, E), bf16),
            vmem((length // BLOCK, BLOCK, E), bf16),
            vmem((length // BLOCK, BLOCK, E), bf16),
            vmem((half * tokens, E), bf16),
            vmem((xs * NY * tokens, width), bf16),
            vmem((g_rows, E), bf16),
            vmem((globals_, E), bf16),
            vmem((globals_, E), bf16),
            vmem(rb.shape, jnp.int32),
            pltpu.SMEM(rb.shape, jnp.int32),
            vmem((half * tokens, columns), f32),
            vmem((g_rows, length), bf16),
            vmem((g_rows, globals_), bf16),
            vmem((g_rows, 1), f32),
            vmem((half * tokens, E), bf16),
            vmem((half * tokens, E), bf16),
            vmem((g_rows, E), bf16),
            vmem((xs, NY, deep, E), bf16),
            vmem((xs, width, deep), bf16),
            vmem((pairs, width, pair), f32),
            vmem((pairs, width // NC, pair), bf16),
            vmem((pairs, width // NC, pair), bf16),
            vmem((pairs, seqs, rows, pair), bf16),
            vmem((pairs, seqs, rows, pair), bf16),
            dma((4,)), dma((4,)), dma((2,)), dma((2,)), dma, dma, dma((4,)), dma((4,)), dma,
            dma, dma, dma((NY,)), dma((NY,)), dma, dma, dma((NY, xs - 1)), dma((NY, xs - 1)),
            dma((pairs,)), dma((pairs,)), dma, dma,
        ],
        compiler_params=pltpu.CompilerParams(
            collective_id=0, has_side_effects=True, vmem_limit_bytes=48 << 20
        ),
        name="layer",
    )(q, k, v, g, f, gq, gk, gv, rb)


def per_device(seqs, xs, features, queries, key_rows, value_rows, cotangent,
               global_queries, global_keys, global_values, random_blocks):
    attended, global_attended, weight_grad = layer(
        seqs, xs, queries, key_rows, value_rows, cotangent, features,
        global_queries, global_keys, global_values, random_blocks,
    )
    return attended[None], global_attended[None], weight_grad


def solution(mesh):
    seqs, xs = mesh.shape["seq"], mesh.shape["dp"] // NC
    long, whole = P("dp", "seq", None), P("dp", None, None)
    return jax.shard_map(
        functools.partial(per_device, seqs, xs),
        mesh=mesh,
        in_specs=(long,) * 5 + (whole,) * 4,
        out_specs=(long, whole, P(("dp", "seq"), None)),
        check_vma=False,
    )
```

time: 168 us -> 127 us (0.76)
  Pallas kernels: 156 us -> 115 us
    pallas_call x3 -> x1, Pallas kernels: 156 us -> 115 us  [layer(): pl.pallas_call(functools.partial(layer_kernel, seqs, xs), out_shape=(shap...]
    unnamed x22 -> x21, local copies, waits for them, and re-layouts: 11.1 us -> 10.9 us
where the time goes in v2:
time: 127 us; the launch traced here: 126 us
  Pallas kernels  115 us (91%)
  local copies, waits for them, and re-layouts  10.9 us (9%)
    pallas_call x1, Pallas kernels, layer(): pl.pallas_call(functools.partial(layer_kernel, seqs, xs), out_shape=(shap...  115 us
    unnamed x21, local copies, waits for them, and re-layouts  10.9 us

profile of v2, /device:TPU:1, one launch (start us, length us, event | category | flops | bytes accessed | tf_op | source)
XLA Modules:
  0.0 126.3 jit_solution(18384596107047658606)
XLA Ops:
  0.6 0.0 copy-start.8
  0.6 0.7 copy-done.8
  1.3 0.0 copy-start
  1.3 1.0 copy-done
  2.4 0.0 copy-start.1
  2.4 1.0 copy-done.1
  3.4 0.0 copy-start.2
  3.4 1.0 copy-done.2
  4.4 0.0 copy-start.3
  4.4 1.0 copy-done.3
  5.5 0.0 copy-start.4
  5.5 1.0 copy-done.4
  6.5 0.0 copy-start.5
  6.5 0.9 copy-done.5
  7.5 0.0 copy-start.6
  7.5 0.9 copy-done.6
  8.4 0.0 copy-start.7
  8.4 0.9 copy-done.7
  9.4 114.8 %layer.1 = (bf16[128,2048]{1,0:T(8,128)(2,1)S(1)}, bf16[64,2048]{1,0:T(8,128)(2,1)S(1)}, f32[8,2048]{1,0:T(8,128)S(1)}) custom-call(bf16[128,2048]{1,0:T(8,128)(2,1)S(1)} %bitcast.8, bf16[2,64,2048]{2,1,0:T(8,128)(2,1)S(1)} %bitcast.9, bf16[2,64,2048]{2,1,0:T(8,128)(2,1)S(1)} %bitcast.10, bf16[128,2048]{1,0:T(8,128)(2,1)S(1)} %bitcast.11, ...), custom_call_target="tpu_custom_call" | custom-call | tf_op jit(solution)/shard_map/layer/pallas_call | solution.py:427
  124.2 0.8 copy.15
  125.0 0.7 copy.16
  125.7 0.6 copy.17
Async XLA Ops:
  0.6 0.7 copy-start.8
  1.3 1.0 copy-start
  2.4 1.0 copy-start.1
  3.4 1.0 copy-start.2
  4.4 1.0 copy-start.3
  5.5 1.0 copy-start.4
  6.5 0.9 copy-start.5
  7.5 0.9 copy-start.6
  8.4 0.9 copy-start.7

commit v3 on v2

--- a/solution.py
+++ b/solution.py
@@ -15,7 +15,7 @@
 NC = 2
 NEGATIVE = -1e30
 MESH = pl.DeviceIdType.MESH
-ANY = pl.BlockSpec(memory_space=pl.ANY)
+HBM = pl.BlockSpec(memory_space=pltpu.HBM)
 
 
 def place(seqs):
@@ -61,7 +61,7 @@
     att_o, gatt_o, w_o = refs[9:12]
     (qs, ks, vs, gs, fs, gqs, gks, gvs, rbv, rbs,
      probs, long_weights, own_weights, mass, att, grad, gatt, grads, turned,
-     total, sib_out, sib_in, part, pieces,
+     total, sib_out, sib_in, x_out, x_in, part, pieces,
      a_send, a_recv, b_send, b_recv, f_send, f_recv, c_send, c_recv, r_sem,
      o_send, o_recv, g_send, g_recv, n_send, n_recv, x_send, x_recv,
      s_send, s_recv, w_send, w_recv) = refs[12:]
@@ -94,19 +94,19 @@
     lax.fori_loop(0, half, greet, 0)
     signal(barrier, sibling, s)
 
-    def greet_f(i, carry):
-        signal(barrier, ((x + i // NY) % xs) * NC + c, z * NY + (y + i) % NY)
-        return carry
-
-    lax.fori_loop(1, xs * NY, greet_f, 0)
+    for i in range(1, NY):
+        signal(barrier, d, z * NY + (y + i) % NY)
+    for i in range(1, xs):
+        signal(barrier, ((x + i) % xs) * NC + c, s)
+    greeted = half + 1 + NY - 1 + xs - 1
 
     @pl.when(mine)
     def _():
-        pl.semaphore_wait(barrier, half + xs * NY - 1)
+        pl.semaphore_wait(barrier, greeted - 1)
 
     @pl.when(others)
     def _():
-        pl.semaphore_wait(barrier, half + xs * NY)
+        pl.semaphore_wait(barrier, greeted)
 
     def spread(n, array, dst):
         def body(i, carry):
@@ -150,17 +150,10 @@
     spread(1, v, vs.at[span(s, own_blocks)])
     spread(3, g, gs.at[span(slot, tokens), :])
 
-    width = fs.shape[1]
-    f_dst = fs.at[span(x * NY + y, tokens), :]
-
-    def send_f(i, carry):
-        to_x, to_y = (x + i // NY) % xs, (y + i) % NY
-        src = f.at[0, :, span(to_x, width)]
-        remote(src, f_dst, f_send, f_recv, to_x * NC + c, z * NY + to_y).start()
-        return carry
-
-    pltpu.make_async_copy(f.at[0, :, span(x, width)], f_dst, f_recv).start()
-    lax.fori_loop(1, xs * NY, send_f, 0)
+    f_dst = fs.at[span(y, tokens), :]
+    pltpu.make_async_copy(f, f_dst, f_recv).start()
+    for i in range(1, NY):
+        remote(f, f_dst, f_send, f_recv, d, z * NY + (y + i) % NY).start()
 
     for n, (_, _, dst) in enumerate(shared):
         arrived(dst, c_recv.at[n])
@@ -243,7 +236,7 @@
     def send_g(i):
         r = flip(y, i)
         to = (c * rows_z + r) * NY + z // NC
-        src, dst = grad.at[span(r, deep), :], grads.at[x, i]
+        src, dst = grad.at[span(r, deep), :], grads.at[i]
         here = jnp.logical_and(owner == c, to == s)
 
         @pl.when(here)
@@ -253,14 +246,6 @@
         @pl.when(jnp.logical_not(here))
         def _():
             remote(src, dst, g_send.at[i], g_recv.at[i], doc, to).start()
-
-    def pass_on(i):
-        arrived(grads.at[x, i], g_recv.at[i])
-        for j in range(1, xs):
-            remote(
-                grads.at[x, i], grads.at[x, i], x_send.at[i, j - 1], x_recv.at[i, j - 1],
-                ((x + j) % xs) * NC + c, s,
-            ).start()
 
     for i in range(NY):
         first = flip(y, i) * per_chunk
@@ -268,8 +253,6 @@
             0, per_chunk, lambda n, a, first=first: backward(first + n, a), 0, unroll=4
         )
         send_g(i)
-        if i > 0:
-            pass_on(i - 1)
 
     def send_o(i, carry):
         r = (i + s) % half
@@ -292,8 +275,6 @@
     sums = dot(long_weights[...], vs[...].reshape(-1, E), NN) + dot(own_weights[...], g_v, NN)
     gatt[...] = (sums / mass[...]).astype(jnp.bfloat16)
 
-    pass_on(NY - 1)
-
     g_dst = gatt_o.at[span(c, g_rows), columns]
 
     def send_n(i, carry):
@@ -313,32 +294,43 @@
     lax.fori_loop(0, seqs, send_n, 0)
 
     arrived(fs, f_recv)
-    for i in range(xs):
-        turned[i] = fs[i * deep : (i + 1) * deep, :].T
+    step = turned.shape[0] // NY
+    for i in range(NY):
+        turned[i * step : (i + 1) * step, :] = fs[:, i * step : (i + 1) * step].T
 
     pairs = NY // 2
     pair = 2 * E
-    rows = sib_in.shape[1]
+    rows = sib_in.shape[2]
     bit = my_row % 2
     for p in range(pairs):
         for i in (2 * p, 2 * p + 1):
-            for j in range(1, xs):
-                arrived(grads.at[(x + xs - j) % xs, i], x_recv.at[i, j - 1])
-        acc = None
-        for source in range(xs):
-            rhs = jnp.concatenate(
-                [grads[source, 2 * p + bit], grads[source, 2 * p + 1 - bit]], axis=1
-            )
-            term = dot(turned[source], rhs, NN)
-            acc = term if acc is None else acc + term
-        total[p] = acc
-        sib_out[p] = total[p, span(1 - c, rows), :].astype(jnp.bfloat16)
+            arrived(grads.at[i], g_recv.at[i])
+        rhs = jnp.concatenate([grads[2 * p + bit], grads[2 * p + 1 - bit]], axis=1)
+        for i in range(xs):
+            slab = turned[i * NC * rows : (i + 1) * NC * rows, :]
+            total[p, i] = dot(slab, rhs, NN)
+            sib_out[p, i] = total[p, i, span(1 - c, rows), :].astype(jnp.bfloat16)
         remote(sib_out.at[p], sib_in.at[p], s_send.at[p], s_recv.at[p], sibling, s).start()
+
+    def chip_sum(p, i):
+        return total[p, i, span(c, rows), :] + sib_in[p, i].astype(jnp.float32)
+
+    for p in range(pairs):
+        arrived(sib_in.at[p], s_recv.at[p])
+        for j in (*range(2, xs), 1)[: xs - 1]:
+            to = (x + j) % xs
+            x_out[p, j - 1] = chip_sum(p, to).astype(jnp.bfloat16)
+            remote(
+                x_out.at[p, j - 1], x_in.at[p, j - 1], x_send.at[p, j - 1], x_recv.at[p, j - 1],
+                to * NC + c, s,
+            ).start()
 
     out_rows = w_o.shape[0]
     for p in range(pairs):
-        arrived(sib_in.at[p], s_recv.at[p])
-        block = total[p, span(c, rows), :] + sib_in[p].astype(jnp.float32)
+        block = chip_sum(p, x)
+        for j in range(1, xs):
+            arrived(x_in.at[p, j - 1], x_recv.at[p, j - 1])
+            block = block + x_in[p, j - 1].astype(jnp.float32)
         part[p] = block.astype(jnp.bfloat16).reshape(seqs, out_rows, pair)
         place_p = (my_row // 2 + p) % pairs
         dst = pieces.at[place_p, s]
@@ -379,17 +371,14 @@
         for n, (_, _, dst) in enumerate(shared):
             arrived(dst, c_send.at[n])
 
-    arrived(fs.at[pl.ds(0, (xs * NY - 1) * tokens), :], f_send)
+    arrived(fs.at[pl.ds(0, (NY - 1) * tokens), :], f_send)
 
     for i in range(NY):
         to = (c * rows_z + flip(y, i)) * NY + z // NC
 
         @pl.when(jnp.logical_not(jnp.logical_and(owner == c, to == s)))
         def _():
-            arrived(grads.at[x, i], g_send.at[i])
-
-        for j in range(1, xs):
-            arrived(grads.at[x, i], x_send.at[i, j - 1])
+            arrived(grads.at[i], g_send.at[i])
 
     @pl.when(mine)
     def _():
@@ -409,6 +398,8 @@
 
     for p in range(pairs):
         arrived(sib_in.at[p], s_send.at[p])
+        for j in range(1, xs):
+            arrived(x_in.at[p, j - 1], x_send.at[p, j - 1])
     arrived(pieces.at[:, pl.ds(0, seqs - 1)], w_send)
 
 
@@ -416,13 +407,13 @@
     tokens, hd, wide = q.shape[1], q.shape[2], f.shape[2]
     half, globals_ = seqs // 2, gk.shape[1]
     rows = wide // (seqs * xs * NC)
-    width, g_rows, pair = wide // xs, globals_ // NC, 2 * E
+    share, g_rows, pair = wide // (xs * NC), globals_ // NC, 2 * E
     pairs, deep, length = NY // 2, NY * tokens, seqs * tokens
     columns = 3 * BLOCK + R * BLOCK + globals_
     shape, vmem, dma = jax.ShapeDtypeStruct, pltpu.VMEM, pltpu.SemaphoreType.DMA
     bf16, f32 = jnp.bfloat16, jnp.float32
     rb = jnp.transpose(rb, (2, 0, 1))
-    q, g = q[0], g[0]
+    q, g, f = q[0], g[0], f[0]
     k, v = (a.reshape(-1, BLOCK, hd) for a in (k, v))
     return pl.pallas_call(
         functools.partial(layer_kernel, seqs, xs),
@@ -431,14 +422,14 @@
             shape((globals_, hd), bf16),
             shape((rows, hd), f32),
         ),
-        in_specs=[ANY] * 9,
-        out_specs=[ANY, ANY, pl.BlockSpec(memory_space=vmem)],
+        in_specs=[HBM] * 9,
+        out_specs=[HBM, HBM, pl.BlockSpec(memory_space=vmem)],
         scratch_shapes=[
             vmem((half * tokens, E), bf16),
             vmem((length // BLOCK, BLOCK, E), bf16),
             vmem((length // BLOCK, BLOCK, E), bf16),
             vmem((half * tokens, E), bf16),
-            vmem((xs * NY * tokens, width), bf16),
+            vmem((deep, wide), bf16),
             vmem((g_rows, E), bf16),
             vmem((globals_, E), bf16),
             vmem((globals_, E), bf16),
@@ -451,19 +442,21 @@
             vmem((half * tokens, E), bf16),
             vmem((half * tokens, E), bf16),
             vmem((g_rows, E), bf16),
-            vmem((xs, NY, deep, E), bf16),
-            vmem((xs, width, deep), bf16),
-            vmem((pairs, width, pair), f32),
-            vmem((pairs, width // NC, pair), bf16),
-            vmem((pairs, width // NC, pair), bf16),
+            vmem((NY, deep, E), bf16),
+            vmem((wide, deep), bf16),
+            vmem((pairs, xs, NC * share, pair), f32),
+            vmem((pairs, xs, share, pair), bf16),
+            vmem((pairs, xs, share, pair), bf16),
+            vmem((pairs, xs - 1, share, pair), bf16),
+            vmem((pairs, xs - 1, share, pair), bf16),
             vmem((pairs, seqs, rows, pair), bf16),
             vmem((pairs, seqs, rows, pair), bf16),
             dma((4,)), dma((4,)), dma((2,)), dma((2,)), dma, dma, dma((4,)), dma((4,)), dma,
-            dma, dma, dma((NY,)), dma((NY,)), dma, dma, dma((NY, xs - 1)), dma((NY, xs - 1)),
+            dma, dma, dma((NY,)), dma((NY,)), dma, dma, dma((pairs, xs - 1)), dma((pairs, xs - 1)),
             dma((pairs,)), dma((pairs,)), dma, dma,
         ],
         compiler_params=pltpu.CompilerParams(
-            collective_id=0, has_side_effects=True, vmem_limit_bytes=48 << 20
+            collective_id=0, has_side_effects=True, vmem_limit_bytes=56 << 20
         ),
         name="layer",
     )(q, k, v, g, f, gq, gk, gv, rb)

time: 127 us -> 112 us (0.88)
  Pallas kernels: 115 us -> 107 us
  local copies, waits for them, and re-layouts: 10.9 us -> 3.42 us
    pallas_call x1, Pallas kernels: 115 us -> 107 us  [layer(): pl.pallas_call(functools.partial(layer_kernel, seqs, xs), out_shape=(shap...]
    unnamed x21 -> x7, local copies, waits for them, and re-layouts: 10.9 us -> 3.42 us
where the time goes in v3:
time: 112 us; the launch traced here: 111 us
  Pallas kernels  107 us (96%)
  local copies, waits for them, and re-layouts  3.42 us (3%)
    pallas_call x1, Pallas kernels, layer(): pl.pallas_call(functools.partial(layer_kernel, seqs, xs), out_shape=(shap...  107 us
    unnamed x7, local copies, waits for them, and re-layouts  3.42 us

profile of v3, /device:TPU:1, one launch (start us, length us, event | category | flops | bytes accessed | tf_op | source)
XLA Modules:
  0.0 111.1 jit_solution(4533312470940384098)
XLA Ops:
  0.6 107.0 %layer.1 = (bf16[128,2048]{1,0:T(8,128)(2,1)}, bf16[64,2048]{1,0:T(8,128)(2,1)}, f32[8,2048]{1,0:T(8,128)}) custom-call(bf16[128,2048]{1,0:T(8,128)(2,1)} %bitcast.9, bf16[2,64,2048]{2,1,0:T(8,128)(2,1)} %bitcast.10, bf16[2,64,2048]{2,1,0:T(8,128)(2,1)} %bitcast.11, bf16[128,2048]{1,0:T(8,128)(2,1)} %bitcast.12, bf16[128,2048]{1,0:T(8,128)(2,1)} %bitcast.13, ...), custom_call_target="tpu_custom_call" | custom-call | tf_op jit(solution)/shard_map/layer/pallas_call | solution.py:418
  107.7 0.0 copy-start
  107.7 1.9 %copy.15 = bf16[1,128,2048]{2,1,0:T(8,128)(2,1)} copy(bf16[1,128,2048]{2,1,0:T(8,128)(2,1)} %bitcast.8) | data formatting | bytes 1048576
  109.6 0.0 copy-done
  109.6 0.0 copy-start.1
  109.6 0.7 copy.16
  110.3 0.2 copy-done.1
  110.5 0.6 copy.17
Async XLA Ops:
  107.7 1.9 %copy-start = (bf16[64,2048]{1,0:T(8,128)(2,1)S(1)}, bf16[64,2048]{1,0:T(8,128)(2,1)}, u32[]{:S(2)}) copy-start(bf16[64,2048]{1,0:T(8,128)(2,1)} %get-tuple-element.7) | copy-start | bytes 786436
  109.6 0.9 copy-start.1

commit v4 on v3

--- a/solution.py
+++ b/solution.py
@@ -60,10 +60,10 @@
     q, k, v, g, f, gq, gk, gv, rb = refs[:9]
     att_o, gatt_o, w_o = refs[9:12]
     (qs, ks, vs, gs, fs, gqs, gks, gvs, rbv, rbs,
-     probs, long_weights, own_weights, mass, att, grad, gatt, grads, turned,
+     probs, dscores, long_weights, own_weights, mass, att, grad, gatt, grads, turned,
      total, sib_out, sib_in, x_out, x_in, part, pieces,
      a_send, a_recv, b_send, b_recv, f_send, f_recv, c_send, c_recv, r_sem,
-     o_send, o_recv, g_send, g_recv, n_send, n_recv, x_send, x_recv,
+     o_send, o_recv, g_send, g_recv, n_send, n_recv, m_send, m_recv, x_send, x_recv,
      s_send, s_recv, w_send, w_recv) = refs[12:]
     d, s, x, c, z, y = place(seqs)
     half = seqs // 2
@@ -108,24 +108,42 @@
     def _():
         pl.semaphore_wait(barrier, greeted)
 
-    def spread(n, array, dst):
+    def send_slice(n, array, dst, sem, h):
+        to = ((h // NY) * NC + c) * NY + h % NY
+        src = array.at[..., head_columns(h)]
+        here = jnp.logical_and(mine, to == s)
+
+        @pl.when(here)
+        def _():
+            pltpu.make_async_copy(src, dst, sem).start()
+
+        @pl.when(jnp.logical_not(here))
+        def _():
+            remote(src, dst, a_send.at[n], sem, x * NC + side, to).start()
+
+    def sent(n, few, count_all, count_few):
+        few = jnp.logical_and(mine, few)
+
+        @pl.when(few)
+        def _():
+            arrived(qs.at[pl.ds(0, count_few * tokens), :], a_send.at[n])
+
+        @pl.when(jnp.logical_not(few))
+        def _():
+            arrived(qs.at[pl.ds(0, count_all * tokens), :], a_send.at[n])
+
+    part_heads = heads // 2
+
+    def spread(n, m, array, dst):
         def body(i, carry):
-            h = (i + s) % heads
-            to = ((h // NY) * NC + c) * NY + h % NY
-            src = array.at[..., head_columns(h)]
-            here = jnp.logical_and(mine, to == s)
-
-            @pl.when(here)
-            def _():
-                pltpu.make_async_copy(src, dst, a_recv.at[n]).start()
-
-            @pl.when(jnp.logical_not(here))
-            def _():
-                remote(src, dst, a_send.at[n], a_recv.at[n], x * NC + side, to).start()
-
+            send_slice(2 * n + m, array, dst, a_recv.at[n, 0], (i + s) % heads)
             return carry
 
-        lax.fori_loop(0, heads, body, 0)
+        lax.fori_loop(m * part_heads, (m + 1) * part_heads, body, 0)
+
+    def spread_sent(n, m):
+        own = ((head + heads - s % heads) % heads) // part_heads
+        sent(2 * n + m, own == m, part_heads, part_heads - 1)
 
     g_rows = gqs.shape[0]
     columns = head_columns(head)
@@ -137,9 +155,9 @@
     )
 
     own_blocks = tokens // BLOCK
-
-    spread(0, k, ks.at[span(s, own_blocks)])
-    spread(2, q, qs.at[span(slot, tokens), :])
+    k_dst, v_dst = ks.at[span(s, own_blocks)], vs.at[span(s, own_blocks)]
+    spread(0, 0, k, k_dst)
+    spread(0, 1, k, k_dst)
 
     @pl.when(owner == c)
     def _():
@@ -147,8 +165,29 @@
             pltpu.make_async_copy(own, dst, c_recv.at[n]).start()
             remote(other, dst, c_send.at[n], c_recv.at[n], sibling, s).start()
 
-    spread(1, v, vs.at[span(s, own_blocks)])
-    spread(3, g, gs.at[span(slot, tokens), :])
+    my_row = z % rows_z
+
+    def spread_step(i):
+        to_y = flip(my_row, i)
+
+        def body(n, carry):
+            h = ((n + z) % (heads // NY)) * NY + to_y
+            send_slice(4 + i, q, qs.at[span(slot, tokens), :], a_recv.at[2, i], h)
+            send_slice(4 + i, g, gs.at[span(slot, tokens), :], a_recv.at[3, i], h)
+            return carry
+
+        lax.fori_loop(0, heads // NY, body, 0)
+
+    def step_sent(i):
+        pieces_all = 2 * (heads // NY)
+        sent(4 + i, flip(my_row, i) == y, pieces_all, pieces_all - 2)
+
+    for m in range(2):
+        spread(1, m, v, v_dst)
+    spread_sent(0, 0)
+    spread_step(0)
+    spread_sent(0, 1)
+    spread_step(1)
 
     f_dst = fs.at[span(y, tokens), :]
     pltpu.make_async_copy(f, f_dst, f_recv).start()
@@ -165,15 +204,19 @@
     own_part, other_part = span(c, count), span(1 - c, count)
 
     def share(n, ref):
-        arrived(ref.at[own_part], a_recv.at[n])
+        arrived(ref.at[own_part], a_recv.at[n, 0])
         remote(ref.at[own_part], ref.at[own_part], b_send.at[n], b_recv.at[n], sibling, s).start()
 
     share(0, ks)
-    arrived(qs, a_recv.at[2])
+    spread_sent(1, 0)
+    if NY > 2:
+        spread_step(2)
     arrived(ks.at[other_part], b_recv.at[0])
 
     g_k, g_v = gks[...], gvs[...]
     width_k = probs.shape[1]
+    per_chunk = count // NY
+    deep = NY * tokens
 
     def listed(ref, b, own):
         first = jnp.clip(b - 1, 0, blocks - 3)
@@ -190,10 +233,8 @@
         valid = (column >= low) & ((column < high) | (column >= 3 * BLOCK))
         scores = jnp.where(valid, scores, NEGATIVE)
         weights = jnp.exp(scores - jnp.max(scores, axis=-1, keepdims=True))
-        probs[span(i, BLOCK), :] = weights / jnp.sum(weights, axis=-1, keepdims=True)
+        probs[span(i % per_chunk, BLOCK), :] = weights / jnp.sum(weights, axis=-1, keepdims=True)
         return carry
-
-    lax.fori_loop(0, count, forward, 0, unroll=4)
 
     g_q = gqs[...]
     long_scores = dot(g_q, ks[...].reshape(-1, E), NT) * scaling
@@ -209,28 +250,48 @@
     long_weights[...] = long_scores.astype(jnp.bfloat16)
     own_weights[...] = own_scores.astype(jnp.bfloat16)
 
+    spread_sent(1, 1)
+    if NY > 3:
+        spread_step(3)
     share(1, vs)
-    arrived(gs, a_recv.at[3])
     arrived(vs.at[other_part], b_recv.at[1])
-
-    per_chunk = count // NY
-    deep = NY * tokens
-    my_row = z % rows_z
-
-    def backward(i, carry):
+    sums = dot(long_weights[...], vs[...].reshape(-1, E), NN) + dot(own_weights[...], g_v, NN)
+    gatt[...] = (sums / mass[...]).astype(jnp.bfloat16)
+
+    g_dst = gatt_o.at[span(c, g_rows), columns]
+    rows_all = seqs // NY
+
+    @pl.when(owner == c)
+    def _():
+        pltpu.make_async_copy(gatt, g_dst, n_recv).start()
+
+    @pl.when(owner != c)
+    def _():
+        remote(gatt, g_dst, n_send, n_recv, doc, s).start()
+
+    for i in range(1, rows_all):
+        remote(gatt, g_dst, n_send, n_recv, doc, ((z + i) % rows_all) * NY + y).start()
+
+
+    def middle(i, carry):
         b = c * count + i
-        rows = span(i, BLOCK)
+        rows, low_rows = span(i, BLOCK), span(i % per_chunk, BLOCK)
         values = listed(vs, b, g_v)
-        p = probs[rows, :]
+        p = probs[low_rows, :]
         g_b = gs[rows, :]
+        dprobs = dot(g_b, values, NT)
         attended = dot(p.astype(jnp.bfloat16), values, NN).astype(jnp.bfloat16)
         delta = jnp.sum(
             g_b.astype(jnp.float32) * attended.astype(jnp.float32), axis=-1, keepdims=True
         )
-        dprobs = dot(g_b, values, NT)
-        dscores = (p * (dprobs - delta)).astype(jnp.bfloat16)
         att[rows, :] = attended
-        grad[rows, :] = (dot(dscores, listed(ks, b, g_k), NN) * scaling).astype(jnp.bfloat16)
+        dscores[low_rows, :] = (p * (dprobs - delta)).astype(jnp.bfloat16)
+        return carry
+
+    def backward(i, carry):
+        ds = dscores[span(i % per_chunk, BLOCK), :]
+        product = dot(ds, listed(ks, c * count + i, g_k), NN)
+        grad[span(i, BLOCK), :] = (product * scaling).astype(jnp.bfloat16)
         return carry
 
     def send_g(i):
@@ -247,13 +308,6 @@
         def _():
             remote(src, dst, g_send.at[i], g_recv.at[i], doc, to).start()
 
-    for i in range(NY):
-        first = flip(y, i) * per_chunk
-        lax.fori_loop(
-            0, per_chunk, lambda n, a, first=first: backward(first + n, a), 0, unroll=4
-        )
-        send_g(i)
-
     def send_o(i, carry):
         r = (i + s) % half
         to = c * half + r
@@ -270,39 +324,28 @@
 
         return carry
 
-    lax.fori_loop(0, half, send_o, 0)
-
-    sums = dot(long_weights[...], vs[...].reshape(-1, E), NN) + dot(own_weights[...], g_v, NN)
-    gatt[...] = (sums / mass[...]).astype(jnp.bfloat16)
-
-    g_dst = gatt_o.at[span(c, g_rows), columns]
-
-    def send_n(i, carry):
-        to = (i + s) % seqs
-        here = jnp.logical_and(owner == c, i == 0)
-
-        @pl.when(here)
-        def _():
-            pltpu.make_async_copy(gatt, g_dst, n_recv).start()
-
-        @pl.when(jnp.logical_not(here))
-        def _():
-            remote(gatt, g_dst, n_send, n_recv, doc, to).start()
-
-        return carry
-
-    lax.fori_loop(0, seqs, send_n, 0)
-
-    arrived(fs, f_recv)
-    step = turned.shape[0] // NY
-    for i in range(NY):
-        turned[i * step : (i + 1) * step, :] = fs[:, i * step : (i + 1) * step].T
+    def chunk(i):
+        r = flip(y, i)
+        arrived(qs.at[span(r, deep), :], a_recv.at[2, i])
+        arrived(gs.at[span(r, deep), :], a_recv.at[3, i])
+        for step in (forward, middle, backward):
+            lax.fori_loop(
+                0, per_chunk, lambda n, a, step=step: step(r * per_chunk + n, a), 0, unroll=True
+            )
+        send_g(i)
 
     pairs = NY // 2
     pair = 2 * E
     rows = sib_in.shape[2]
     bit = my_row % 2
-    for p in range(pairs):
+
+    def turn():
+        arrived(fs, f_recv)
+        size = turned.shape[0] // NY
+        for i in range(NY):
+            turned[i * size : (i + 1) * size, :] = fs[:, i * size : (i + 1) * size].T
+
+    def product(p):
         for i in (2 * p, 2 * p + 1):
             arrived(grads.at[i], g_recv.at[i])
         rhs = jnp.concatenate([grads[2 * p + bit], grads[2 * p + 1 - bit]], axis=1)
@@ -315,7 +358,7 @@
     def chip_sum(p, i):
         return total[p, i, span(c, rows), :] + sib_in[p, i].astype(jnp.float32)
 
-    for p in range(pairs):
+    def along_x(p):
         arrived(sib_in.at[p], s_recv.at[p])
         for j in (*range(2, xs), 1)[: xs - 1]:
             to = (x + j) % xs
@@ -326,22 +369,47 @@
             ).start()
 
     out_rows = w_o.shape[0]
-    for p in range(pairs):
+
+    def scatter(p):
         block = chip_sum(p, x)
         for j in range(1, xs):
             arrived(x_in.at[p, j - 1], x_recv.at[p, j - 1])
             block = block + x_in[p, j - 1].astype(jnp.float32)
         part[p] = block.astype(jnp.bfloat16).reshape(seqs, out_rows, pair)
-        place_p = (my_row // 2 + p) % pairs
-        dst = pieces.at[place_p, s]
+        dst = pieces.at[(my_row // 2 + p) % pairs, s]
         pltpu.make_async_copy(part.at[p, s], dst, w_recv).start()
 
-        def send_w(i, carry, p=p, dst=dst):
+        def send_w(i, carry):
             to = (i + s) % seqs
             remote(part.at[p, to], dst, w_send, w_recv, d, to).start()
             return carry
 
         lax.fori_loop(1, seqs, send_w, 0)
+
+    for i in range(NY - 1):
+        chunk(i)
+    if pairs > 1:
+        turn()
+        product(0)
+    chunk(NY - 1)
+    if pairs > 1:
+        along_x(0)
+    else:
+        turn()
+
+    group = att_o.shape[1] // NY
+    arrived(gatt_o.at[:, pl.ds(0, group)], n_recv)
+    for n in range(heads // NY):
+        ref = gatt_o.at[:, head_columns(n * NY + y)]
+        for i in range(1, NY):
+            remote(ref, ref, m_send, m_recv, d, z * NY + (y + i) % NY).start()
+
+    product(pairs - 1)
+    lax.fori_loop(0, half, send_o, 0)
+    if pairs > 1:
+        scatter(0)
+    along_x(pairs - 1)
+    scatter(pairs - 1)
 
     arrived(pieces, w_recv)
     for n in range(NY):
@@ -353,16 +421,10 @@
             w_o[:, start : start + pair] = acc
 
     arrived(att_o, o_recv)
-    arrived(gatt_o, n_recv)
-
-    for n in range(4):
-        @pl.when(mine)
-        def _():
-            arrived(qs.at[pl.ds(0, (half - 1) * tokens), :], a_send.at[n])
-
-        @pl.when(others)
-        def _():
-            arrived(qs, a_send.at[n])
+    arrived(gatt_o.at[:, pl.ds(0, (NY - 1) * group)], m_recv)
+
+    for i in range(NY):
+        step_sent(i)
     for n, ref in enumerate((ks, vs)):
         arrived(ref.at[own_part], b_send.at[n])
 
@@ -390,12 +452,13 @@
 
     @pl.when(owner == c)
     def _():
-        arrived(att.at[pl.ds(0, (seqs - 1) * g_rows), :], n_send)
+        arrived(att.at[pl.ds(0, (rows_all - 1) * g_rows), :], n_send)
 
     @pl.when(owner != c)
     def _():
-        arrived(att.at[pl.ds(0, seqs * g_rows), :], n_send)
-
+        arrived(att.at[pl.ds(0, rows_all * g_rows), :], n_send)
+
+    arrived(gatt_o.at[:, pl.ds(0, (NY - 1) * group)], m_send)
     for p in range(pairs):
         arrived(sib_in.at[p], s_send.at[p])
         for j in range(1, xs):
@@ -435,7 +498,8 @@
             vmem((globals_, E), bf16),
             vmem(rb.shape, jnp.int32),
             pltpu.SMEM(rb.shape, jnp.int32),
-            vmem((half * tokens, columns), f32),
+            vmem((half * tokens // NY, columns), f32),
+            vmem((half * tokens // NY, columns), bf16),
             vmem((g_rows, length), bf16),
             vmem((g_rows, globals_), bf16),
             vmem((g_rows, 1), f32),
@@ -451,8 +515,8 @@
             vmem((pairs, xs - 1, share, pair), bf16),
             vmem((pairs, seqs, rows, pair), bf16),
             vmem((pairs, seqs, rows, pair), bf16),
-            dma((4,)), dma((4,)), dma((2,)), dma((2,)), dma, dma, dma((4,)), dma((4,)), dma,
-            dma, dma, dma((NY,)), dma((NY,)), dma, dma, dma((pairs, xs - 1)), dma((pairs, xs - 1)),
+            dma((4 + NY,)), dma((4, NY)), dma((2,)), dma((2,)), dma, dma, dma((4,)), dma((4,)), dma,
+            dma, dma, dma((NY,)), dma((NY,)), dma, dma, dma, dma, dma((pairs, xs - 1)), dma((pairs, xs - 1)),
             dma((pairs,)), dma((pairs,)), dma, dma,
         ],
         compiler_params=pltpu.CompilerParams(
@@ -462,12 +526,37 @@
     )(q, k, v, g, f, gq, gk, gv, rb)
 
 
+def deliver_kernel(*refs):
+    count = (len(refs) - 1) // 2
+    copies = [
+        pltpu.make_async_copy(refs[n], refs[count + n], refs[-1].at[n]) for n in range(count)
+    ]
+    for copy in copies:
+        copy.start()
+    for copy in copies:
+        copy.wait()
+
+
+def deliver(*arrays):
+    count = len(arrays)
+    return pl.pallas_call(
+        deliver_kernel,
+        out_shape=[jax.ShapeDtypeStruct(a.shape, a.dtype) for a in arrays],
+        in_specs=[HBM] * count,
+        out_specs=[HBM] * count,
+        scratch_shapes=[pltpu.SemaphoreType.DMA((count,))],
+        compiler_params=pltpu.CompilerParams(vmem_limit_bytes=56 << 20),
+        name="deliver",
+    )(*arrays)
+
+
 def per_device(seqs, xs, features, queries, key_rows, value_rows, cotangent,
                global_queries, global_keys, global_values, random_blocks):
     attended, global_attended, weight_grad = layer(
         seqs, xs, queries, key_rows, value_rows, cotangent, features,
         global_queries, global_keys, global_values, random_blocks,
     )
+    attended, global_attended, weight_grad = deliver(attended, global_attended, weight_grad)
     return attended[None], global_attended[None], weight_grad
 
 

time: 112 us -> 131 us (1.17)
  Pallas kernels: 107 us -> 130 us
  local copies, waits for them, and re-layouts: 3.42 us -> 0 us
    pallas_call x0 -> x1, Pallas kernels: none -> 26.9 us  [deliver(): pl.pallas_call(deliver_kernel, out_shape=[jax.ShapeDtypeStruct(a.shape, a...]
    pallas_call x1, Pallas kernels: 107 us -> 103 us  [layer(): pl.pallas_call(functools.partial(layer_kernel, seqs, xs), out_shape=(shap...]
    unnamed x7 -> x0, local copies, waits for them, and re-layouts: 3.42 us -> none
where the time goes in v4:
time: 131 us
  Pallas kernels  130 us (99%)
    pallas_call x1, Pallas kernels, layer(): pl.pallas_call(functools.partial(layer_kernel, seqs, xs), out_shape=(shap...  103 us
    pallas_call x1, Pallas kernels, deliver(): pl.pallas_call(deliver_kernel, out_shape=[jax.ShapeDtypeStruct(a.shape, a...  26.9 us

profile of v4, /device:TPU:1, one launch (start us, length us, event | category | flops | bytes accessed | tf_op | source)
XLA Modules:
  0.0 130.8 jit_solution(16219573976369641396)
XLA Ops:
  0.6 103.3 %layer.1 = (bf16[128,2048]{1,0:T(8,128)(2,1)}, bf16[64,2048]{1,0:T(8,128)(2,1)}, f32[8,2048]{1,0:T(8,128)}) custom-call(bf16[128,2048]{1,0:T(8,128)(2,1)} %bitcast.8, bf16[2,64,2048]{2,1,0:T(8,128)(2,1)} %bitcast.9, bf16[2,64,2048]{2,1,0:T(8,128)(2,1)} %bitcast.10, bf16[128,2048]{1,0:T(8,128)(2,1)} %bitcast.11, bf16[128,2048]{1,0:T(8,128)(2,1)} %bitcast.12, ...), custom_call_target="tpu_custom_call" | custom-call | tf_op jit(solution)/shard_map/layer/pallas_call | solution.py:481
  103.9 26.9 %deliver.1 = (bf16[128,2048]{1,0:T(8,128)(2,1)}, bf16[64,2048]{1,0:T(8,128)(2,1)}, f32[8,2048]{1,0:T(8,128)}) custom-call(bf16[128,2048]{1,0:T(8,128)(2,1)} %get-tuple-element.9.refs_0_, bf16[64,2048]{1,0:T(8,128)(2,1)} %get-tuple-element.10.refs_1_, f32[8,2048]{1,0:T(8,128)} %get-tuple-element.11.refs_2_), custom_call_target="tpu_custom_call" | custom-call | tf_op jit(solution)/shard_map/deliver/pallas_call | solution.py:542

commit v5 on v4

--- a/solution.py
+++ b/solution.py
@@ -184,10 +184,10 @@
 
     for m in range(2):
         spread(1, m, v, v_dst)
+    spread_step(0)
     spread_sent(0, 0)
-    spread_step(0)
+    spread_step(1)
     spread_sent(0, 1)
-    spread_step(1)
 
     f_dst = fs.at[span(y, tokens), :]
     pltpu.make_async_copy(f, f_dst, f_recv).start()
@@ -527,24 +527,18 @@
 
 
 def deliver_kernel(*refs):
-    count = (len(refs) - 1) // 2
-    copies = [
-        pltpu.make_async_copy(refs[n], refs[count + n], refs[-1].at[n]) for n in range(count)
-    ]
-    for copy in copies:
-        copy.start()
-    for copy in copies:
-        copy.wait()
+    count = len(refs) // 2
+    for n in range(count):
+        refs[count + n][...] = refs[n][...]
 
 
 def deliver(*arrays):
-    count = len(arrays)
+    vmem = pl.BlockSpec(memory_space=pltpu.VMEM)
     return pl.pallas_call(
         deliver_kernel,
         out_shape=[jax.ShapeDtypeStruct(a.shape, a.dtype) for a in arrays],
-        in_specs=[HBM] * count,
-        out_specs=[HBM] * count,
-        scratch_shapes=[pltpu.SemaphoreType.DMA((count,))],
+        in_specs=[vmem] * len(arrays),
+        out_specs=[vmem] * len(arrays),
         compiler_params=pltpu.CompilerParams(vmem_limit_bytes=56 << 20),
         name="deliver",
     )(*arrays)

time: 131 us -> 106 us (0.81)
  Pallas kernels: 130 us -> 105 us
    pallas_call x1, Pallas kernels: 26.9 us -> 2.03 us  [deliver(): pl.pallas_call(deliver_kernel, out_shape=[jax.ShapeDtypeStruct(a.shape, a...]
where the time goes in v5:
time: 106 us; the launch traced here: 105 us
  Pallas kernels  105 us (99%)
    pallas_call x1, Pallas kernels, layer(): pl.pallas_call(functools.partial(layer_kernel, seqs, xs), out_shape=(shap...  103 us

profile of v5, /device:TPU:1, one launch (start us, length us, event | category | flops | bytes accessed | tf_op | source)
XLA Modules:
  0.0 105.5 jit_solution(9248139785945603154)
XLA Ops:
  0.6 102.8 %layer.1 = (bf16[128,2048]{1,0:T(8,128)(2,1)}, bf16[64,2048]{1,0:T(8,128)(2,1)}, f32[8,2048]{1,0:T(8,128)}) custom-call(bf16[128,2048]{1,0:T(8,128)(2,1)} %bitcast.8, bf16[2,64,2048]{2,1,0:T(8,128)(2,1)} %bitcast.9, bf16[2,64,2048]{2,1,0:T(8,128)(2,1)} %bitcast.10, bf16[128,2048]{1,0:T(8,128)(2,1)} %bitcast.11, bf16[128,2048]{1,0:T(8,128)(2,1)} %bitcast.12, ...), custom_call_target="tpu_custom_call" | custom-call | tf_op jit(solution)/shard_map/layer/pallas_call | solution.py:481
  103.4 2.0 %deliver.1 = (bf16[128,2048]{1,0:T(8,128)(2,1)}, bf16[64,2048]{1,0:T(8,128)(2,1)}, f32[8,2048]{1,0:T(8,128)}) custom-call(bf16[128,2048]{1,0:T(8,128)(2,1)} %get-tuple-element.9.refs_0_, bf16[64,2048]{1,0:T(8,128)(2,1)} %get-tuple-element.10.refs_1_, f32[8,2048]{1,0:T(8,128)} %get-tuple-element.11.refs_2_), custom_call_target="tpu_custom_call" | custom-call | tf_op jit(solution)/shard_map/deliver/pallas_call | solution.py:537
